TPU v7x, 32 devices: a whole 2x2x4 slice. The times are simulated.
32 devices in a mesh: phase: 2 (over x), dp: 4 (over y, core), mp: 4 (over z).
Axes of the slice: x: 2, y: 2, z: 4, core: 2. Of those that a mesh axis runs over, the one named last changes fastest.
Arguments:
- memory: bfloat16 [4, 256, 1024], P('dp', None, 'mp'), may hold values from -6 to 6
- states: bfloat16 [2, 4, 256, 1024], P('phase', 'dp', None, 'mp'), may hold values from -6 to 6
- targets: bfloat16 [2, 4, 256, 1024], P('phase', 'dp', None, 'mp'), may hold values from -6 to 6
- w_query: bfloat16 [2, 1024, 16384], P('phase', None, 'mp'), may hold values from -0.1875 to 0.1875
- w_key: bfloat16 [2, 1024, 16384], P('phase', None, 'mp'), may hold values from -0.1875 to 0.1875
- w_value: bfloat16 [2, 1024, 16384], P('phase', None, 'mp'), may hold values from -0.1875 to 0.1875
- w_out: bfloat16 [2, 16384, 1024], P('phase', 'mp'), may hold values from -0.046875 to 0.046875
- src_ids: int32 [4, 256], P('dp'), may hold values from 0 to 3, never falling along the last dimension, each value on 1 to 128 neighbouring positions
- tgt_ids: int32 [4, 256], P('dp'), may hold values from 0 to 3, never falling along the last dimension, each value on 1 to 128 neighbouring positions
- counts: int32 [4], P('dp'), may hold values from 1 to 256
Outputs:
- cross_out: bfloat16 [2, 4, 256, 1024], P('phase', 'dp', None, 'mp')
- loss: float32 [2], P('phase')
- states_grad: bfloat16 [2, 4, 256, 1024], P('phase', 'dp', None, 'mp')
- memory_grad: bfloat16 [4, 256, 1024], P('dp', None, 'mp')
Inputs may be any that keep to these rules, and one draw needn't show every extreme that they name: `src_ids`: both id arrays of a sample hold all segment numbers 0 to 3.
All inputs are finite; a program needn't handle non-finite values.
Results may differ from a plain program's by a relative error of at most 0.013.
The roundings to bfloat16 on the way count: a program that leaves them out, or rounds other values in their place, can miss the bound.
Values may be sent and summed in bfloat16 or wider, within the bound.
No kernel may reach another device: no remote copies, remote signals or barrier semaphores. Data moves between devices by JAX's collectives and lax.ppermute only.
A program may use at most 128 MiB of HBM per device.

v0:
```python
import jax
import jax.numpy as jnp
from jax import lax
from jax.sharding import PartitionSpec as P

HEAD = 128


def local(memory, states, targets, w_query, w_key, w_value, w_out, src_ids, tgt_ids, counts):
    count_local = jnp.sum(counts.astype(jnp.float32))
    mem_all, state_all, target_all = (
        lax.all_gather(memory, "mp", axis=2, tiled=True),
        lax.all_gather(states[0], "mp", axis=2, tiled=True),
        lax.all_gather(targets[0], "mp", axis=2, tiled=True),
    )
    wq = w_query[0]
    wk = w_key[0]
    wv = w_value[0]
    wo = w_out[0]
    batch = mem_all.shape[0]
    src_len = mem_all.shape[1]
    tgt_len = state_all.shape[1]
    local_inner = wq.shape[1]
    local_heads = local_inner // HEAD
    query = jnp.einsum("btd,dk->btk", state_all, wq, preferred_element_type=jnp.float32).astype(
        jnp.bfloat16
    )
    keys = jnp.einsum("bjd,dk->bjk", mem_all, wk, preferred_element_type=jnp.float32).astype(
        jnp.bfloat16
    )
    values = jnp.einsum("bjd,dk->bjk", mem_all, wv, preferred_element_type=jnp.float32).astype(
        jnp.bfloat16
    )
    query_h = query.reshape(batch, tgt_len, local_heads, HEAD)
    keys_h = keys.reshape(batch, src_len, local_heads, HEAD)
    values_h = values.reshape(batch, src_len, local_heads, HEAD)
    scores = jnp.einsum("bthe,bjhe->bhtj", query_h, keys_h, preferred_element_type=jnp.float32)
    allowed = tgt_ids[:, None, :, None] == src_ids[:, None, None, :]
    scores = jnp.where(allowed, scores, -1e30)
    probs = jax.nn.softmax(scores, axis=-1)
    probs_low = probs.astype(jnp.bfloat16)
    attended = jnp.einsum(
        "bhtj,bjhe->bthe", probs_low, values_h, preferred_element_type=jnp.float32
    )
    attended = attended.astype(jnp.bfloat16).reshape(batch, tgt_len, local_inner)
    out_part = jnp.einsum("btk,kd->btd", attended, wo, preferred_element_type=jnp.float32)
    valid = (jnp.arange(tgt_len)[None, :] < counts[:, None]).astype(jnp.bfloat16)
    grad_out = target_all * valid[:, :, None]
    grad_att = jnp.einsum("btd,kd->btk", grad_out, wo, preferred_element_type=jnp.float32)
    grad_att = grad_att.astype(jnp.bfloat16).reshape(batch, tgt_len, local_heads, HEAD)
    grad_prob = jnp.einsum(
        "bthe,bjhe->bhtj", grad_att, values_h, preferred_element_type=jnp.float32
    )
    inner = jnp.sum(probs * grad_prob, axis=-1, keepdims=True)
    grad_score = (probs * (grad_prob - inner)).astype(jnp.bfloat16)
    grad_q = jnp.einsum("bhtj,bjhe->bthe", grad_score, keys_h, preferred_element_type=jnp.float32)
    grad_q = grad_q.astype(jnp.bfloat16).reshape(batch, tgt_len, local_inner)
    grad_k = jnp.einsum("bhtj,bthe->bjhe", grad_score, query_h, preferred_element_type=jnp.float32)
    grad_k = grad_k.astype(jnp.bfloat16).reshape(batch, src_len, local_inner)
    grad_v = jnp.einsum("bhtj,bthe->bjhe", probs_low, grad_att, preferred_element_type=jnp.float32)
    grad_v = grad_v.astype(jnp.bfloat16).reshape(batch, src_len, local_inner)
    grad_x_part = jnp.einsum("btk,dk->btd", grad_q, wq, preferred_element_type=jnp.float32)
    grad_m_part = jnp.einsum("bjk,dk->bjd", grad_k, wk, preferred_element_type=jnp.float32)
    grad_m_part = grad_m_part + jnp.einsum(
        "bjk,dk->bjd", grad_v, wv, preferred_element_type=jnp.float32
    )
    out_sum = lax.psum_scatter(out_part, "mp", scatter_dimension=2, tiled=True)
    grad_x, grad_m = (
        lax.psum_scatter(grad_x_part, "mp", scatter_dimension=2, tiled=True),
        lax.psum_scatter(grad_m_part, "mp", scatter_dimension=2, tiled=True),
    )
    out_low = out_sum.astype(jnp.bfloat16)
    grad_local = targets[0] * valid[:, :, None]
    loss_part = jnp.sum(out_low.astype(jnp.float32) * grad_local.astype(jnp.float32))
    loss_total, count_total = lax.psum((loss_part, count_local / lax.axis_size("mp")), ("dp", "mp"))
    grad_mem = lax.psum(grad_m, "phase")
    loss = (loss_total / count_total).reshape(1)
    states_grad = (grad_x / count_total).astype(jnp.bfloat16)[None]
    memory_grad = (grad_mem / count_total).astype(jnp.bfloat16)
    return (out_low[None], loss, states_grad, memory_grad)


def solution(mesh):
    placed = (
        P("dp", None, "mp"),
        P("phase", "dp", None, "mp"),
        P("phase", "dp", None, "mp"),
        P("phase", None, "mp"),
        P("phase", None, "mp"),
        P("phase", None, "mp"),
        P("phase", "mp", None),
        P("dp", None),
        P("dp", None),
        P("dp"),
    )
    return jax.shard_map(
        local,
        mesh=mesh,
        in_specs=placed,
        out_specs=(
            P("phase", "dp", None, "mp"),
            P("phase"),
            P("phase", "dp", None, "mp"),
            P("dp", None, "mp"),
        ),
        check_vma=False,
    )
```

profile of v0, /device:TPU:0, one launch (start us, length us, event | category | flops | bytes accessed | tf_op | source)
XLA Modules:
  0.0 245.4 jit_solution(11665159533606123503)
XLA Ops:
  7.9 17.6 %all_gather.9 = bf16[1,256,1024]{2,1,0:T(8,128)(2,1)S(1)} all-gather(bf16[1,256,256]{2,1,0:T(8,128)(2,1)} %param.10), channel_id=1, replica_groups=mesh['phase'=2,'dp'=4,'mp'=4] {'mp'}, dimensions={2}, use_global_device_ids=true | all-gather | bytes 655360 | tf_op jit(solution)/shard_map/all_gather | solution.py:12
  25.5 16.6 %all-gather = bf16[1,1,256,1024]{3,2,1,0:T(8,128)(2,1)S(1)} all-gather(bf16[1,1,256,256]{3,2,1,0:T(8,128)(2,1)} %param.11), channel_id=2, replica_groups=mesh['phase'=2,'dp'=4,'mp'=4] {'mp'}, dimensions={3}, use_global_device_ids=true | all-gather | bytes 655360 | tf_op jit(solution)/shard_map/all_gather | solution.py:13
  42.0 5.7 %fusion.23 = bf16[256,4096]{1,0:T(8,128)(2,1)S(1)} fusion(bf16[1,1024,4096]{2,1,0:T(8,128)(2,1)} %param.13, bf16[1,1,256,1024]{3,2,1,0:T(8,128)(2,1)S(1)} %all-gather), kind=kOutput, calls=%fused_computation.23 | convolution fusion | flops 2148532224 | bytes 11010048 | tf_op jit(solution)/shard_map/btd,dk->btk/dot_general | solution.py:25
  47.7 2.5 %copy.30 = bf16[256,4096]{0,1:T(8,128)(2,1)} copy(bf16[256,4096]{1,0:T(8,128)(2,1)S(1)} %fusion.23) | data formatting | bytes 4194304 | tf_op jit(solution)/shard_map/reshape.18
  50.2 7.1 %fusion.51 = bf16[32,32,8,128]{3,2,1,0:T(8,128)(2,1)} fusion(bf16[1,1024,4096]{2,1,0:T(8,128)(2,1)} %param.15, bf16[1,256,1024]{2,1,0:T(8,128)(2,1)S(1)} %all_gather.9), kind=kOutput, calls=%fused_computation.42 | convolution fusion | flops 2148532224 | bytes 11010048 | tf_op jit(solution)/shard_map/bjd,dk->bjk/dot_general | solution.py:31
  57.3 7.0 %fusion.26 = bf16[256,4096]{1,0:T(8,128)(2,1)} fusion(bf16[1,1024,4096]{2,1,0:T(8,128)(2,1)} %param.14, bf16[1,256,1024]{2,1,0:T(8,128)(2,1)S(1)} %all_gather.9), kind=kOutput, calls=%fused_computation.24 | convolution fusion | flops 2148532224 | bytes 11010048 | tf_op jit(solution)/shard_map/bjd,dk->bjk/dot_general | solution.py:28
  64.3 3.3 %copy.31 = bf16[256,4096]{0,1:T(8,128)(2,1)S(1)} copy(bf16[256,4096]{1,0:T(8,128)(2,1)} %fusion.26) | data formatting | bytes 4194304 | tf_op jit(solution)/shard_map/reshape.19
  67.6 15.5 %all-gather.1 = bf16[1,1,256,1024]{3,2,1,0:T(8,128)(2,1)S(1)} all-gather(bf16[1,1,256,256]{3,2,1,0:T(8,128)(2,1)S(1)} %copy-done.4), channel_id=3, replica_groups=mesh['phase'=2,'dp'=4,'mp'=4] {'mp'}, dimensions={3}, use_global_device_ids=true | all-gather | bytes 655360 | tf_op jit(solution)/shard_map/all_gather | solution.py:14
  83.1 7.1 %fusion.29 = bf16[256,4096]{1,0:T(8,128)(2,1)} fusion(bf16[1,4096,1024]{2,1,0:T(8,128)(2,1)} %param.16, bf16[1,1,256,1024]{3,2,1,0:T(8,128)(2,1)S(1)} %all-gather.1, bf16[256]{0:T(256)(128)(2,1)S(1)} %compare_convert_fusion), kind=kOutput, calls=%fused_computation.25 | convolution fusion | flops 2148794368 | bytes 11010560 | tf_op jit(solution)/shard_map/btd,kd->btk/dot_general | solution.py:49
  90.2 4.1 %copy.32 = bf16[256,4096]{0,1:T(8,128)(2,1)} copy(bf16[256,4096]{1,0:T(8,128)(2,1)} %fusion.29) | data formatting | bytes 4194304 | tf_op jit(solution)/shard_map/reshape.38
  94.5 7.6 %fusion.75 = (f32[32,256]{1,0:T(8,128)S(1)}, f32[32,256,256]{1,2,0:T(8,128)}) fusion(pred[256,256]{0,1:T(8,128)(4,1)S(1)} %broadcast_compare_fusion, bf16[256,32,128]{0,2,1:T(8,128)(2,1)} %bitcast.124, bf16[256,32,128]{0,2,1:T(8,128)(2,1)S(1)} %bitcast.122), kind=kOutput, calls=%fused_computation.63 | convolution fusion | flops 543162624 | bytes 12681216 | tf_op jit(solution)/shard_map/sub | solution.py:40
  102.0 7.0 %fusion.41 = bf16[32,128,256]{2,1,0:T(8,128)(2,1)} fusion(bf16[256,32,128]{0,2,1:T(8,128)(2,1)} %bitcast.127, f32[32,256,256]{1,2,0:T(8,128)} %get-tuple-element.9, f32[32,256]{1,0:T(8,128)S(1)} %get-tuple-element.8), kind=kOutput, calls=%fused_computation.36 | convolution fusion | flops 542113792 | bytes 12615680 | tf_op jit(solution)/shard_map/bhtj,bthe->bjhe/dot_general | solution.py:60
  115.8 6.5 %fusion.5 = f32[256,1024]{1,0:T(8,128)S(1)} fusion(bf16[256,4096]{0,1:T(8,128)(2,1)S(1)} %bitcast.130, bf16[1,1024,4096]{2,1,0:T(8,128)(2,1)} %param.14), kind=kOutput, calls=%fused_computation.5 | convolution fusion | flops 2147483648 | bytes 11534336 | tf_op jit(solution)/shard_map/bjk,dk->bjd/dot_general | solution.py:63
  122.3 3.4 %fusion.63 = f32[1,256,1024]{2,1,0:T(8,128)} fusion(f32[256,1024]{1,0:T(8,128)S(1)} %fusion.5, bf16[256,4096]{0,1:T(8,128)(2,1)S(1)} %bitcast.135, bf16[1,1024,4096]{2,1,0:T(8,128)(2,1)S(1)} %bitcast.134), kind=kOutput, calls=%fused_computation.46 | convolution fusion | flops 2147745792 | bytes 12582912 | tf_op jit(solution)/shard_map/bjk,dk->bjd/dot_general | solution.py:64
  126.0 5.0 %fusion.44 = bf16[32,128,256]{2,1,0:T(8,128)(2,1)S(1)} fusion(bf16[32,32,8,128]{3,2,1,0:T(8,128)(2,1)} %fusion.51, f32[32,256,256]{1,2,0:T(8,128)} %get-tuple-element.9, f32[32,256]{1,0:T(8,128)S(1)} %get-tuple-element.8), kind=kOutput, calls=%fused_computation.37 | convolution fusion | flops 542113792 | bytes 12615680 | tf_op jit(solution)/shard_map/bhtj,bjhe->bthe/dot_general | solution.py:42
  131.1 7.0 %fusion.57 = f32[1,256,1024]{2,1,0:T(8,128)} fusion(bf16[256,4096]{0,1:T(8,128)(2,1)S(1)} %bitcast.126, bf16[1,4096,1024]{2,1,0:T(8,128)(2,1)} %param.16), kind=kOutput, calls=%fused_computation.44 | convolution fusion | flops 2147483648 | bytes 11534336 | tf_op jit(solution)/shard_map/btk,kd->btd/dot_general | solution.py:46
  138.2 2.9 %convolution_convert_fusion.1 = bf16[32,128,256]{2,1,0:T(8,128)(2,1)S(1)} fusion(bf16[256,32,128]{0,2,1:T(8,128)(2,1)S(1)} %bitcast.123, bf16[32,256,256]{1,2,0:T(8,128)(2,1)} %copy-done), kind=kOutput, calls=%fused_computation.39 | convolution fusion | flops 537919488 | bytes 8388608 | tf_op jit(solution)/shard_map/bhtj,bjhe->bthe/dot_general | solution.py:56
  141.1 6.8 %fusion.54 = f32[1,256,1024]{2,1,0:T(8,128)} fusion(bf16[256,4096]{0,1:T(8,128)(2,1)S(1)} %bitcast.129, bf16[1,1024,4096]{2,1,0:T(8,128)(2,1)} %param.13), kind=kOutput, calls=%fused_computation.43 | convolution fusion | flops 2147483648 | bytes 11534336 | tf_op jit(solution)/shard_map/btk,dk->btd/dot_general | solution.py:62
  148.0 6.4 %reduce-scatter.8.cloned.1.call-done = f32[1,256,256]{2,1,0:T(8,128)} async-done(((f32[1,256,1024]{2,1,0:T(8,128)}), f32[1,256,256]{2,1,0:T(8,128)}) %reduce-scatter.8.cloned.1.call-update) | async-done | bytes 262160 | tf_op jit(solution)/shard_map/reduce_scatter | solution.py:70
  154.4 28.1 %reduce-scatter.4.cloned.1.call-done = f32[1,256,256]{2,1,0:T(8,128)} async-done(((f32[1,256,1024]{2,1,0:T(8,128)}), f32[1,256,256]{2,1,0:T(8,128)}) %reduce-scatter.4.cloned.1.call-update) | async-done | bytes 262160 | tf_op jit(solution)/shard_map/reduce_scatter | solution.py:67
  184.7 32.6 %all-reduce = (f32[]{:T(128)}, f32[]{:T(128)}) all-reduce(f32[]{:T(128)} %get-tuple-element.6, f32[]{:T(128)} %bitcast.15), channel_id=1, replica_groups=mesh['phase'=2,'dp'=4,'mp'=4] {'dp','mp'}, use_global_device_ids=true, to_apply=%region_4.5 | all-reduce | flops 2 | bytes 16 | tf_op jit(solution)/shard_map/psum | solution.py:75
  218.7 2.3 fusion.73
  220.9 14.5 %all-reduce.3.cloned.1.call-done = f32[1,256,256]{2,1,0:T(8,128)} async-done(((f32[1,256,256]{2,1,0:T(8,128)}), f32[1,256,256]{2,1,0:T(8,128)}) %all-reduce.3.cloned.1.call-update) | async-done | bytes 262160 | tf_op jit(solution)/shard_map/psum | solution.py:76
  235.4 2.3 divide_convert_fusion
  (38 shorter events, 9.5 us)
Async XLA Ops:
  7.2 147.2 %reduce-scatter.8.cloned.1.call-start = ((), (), s32[]{:S(2)}) async-start(), calls=%async_computation.5 | async-start | bytes 1310720 | tf_op jit(solution)/shard_map/reduce_scatter | solution.py:70
  64.3 3.3 %copy-start.4 = (bf16[1,1,256,256]{3,2,1,0:T(8,128)(2,1)S(1)}, bf16[1,1,256,256]{3,2,1,0:T(8,128)(2,1)}, u32[]{:S(2)}) copy-start(bf16[1,1,256,256]{3,2,1,0:T(8,128)(2,1)} %param.12) | copy-start | bytes 393220
  90.2 4.1 %copy-start.5 = (s32[1,256]{1,0:T(1,128)S(1)}, s32[1,256]{1,0:T(1,128)}, u32[]{:S(2)}) copy-start(s32[1,256]{1,0:T(1,128)} %param.18) | copy-start | bytes 3076
  90.2 4.1 %copy-start.6 = (s32[1,256]{1,0:T(1,128)S(1)}, s32[1,256]{1,0:T(1,128)}, u32[]{:S(2)}) copy-start(s32[1,256]{1,0:T(1,128)} %param.17) | copy-start | bytes 3076
  102.0 7.0 %copy-start.1 = (f32[32,256,256]{1,2,0:T(8,128)S(1)}, f32[32,256,256]{1,2,0:T(8,128)}, u32[]{:S(2)}) copy-start(f32[32,256,256]{1,2,0:T(8,128)} %get-tuple-element.9) | copy-start | bytes 25165828
  102.0 7.7 %copy-start.3 = (bf16[256,4096]{0,1:T(8,128)(2,1)S(1)}, bf16[256,4096]{0,1:T(8,128)(2,1)}, u32[]{:S(2)}) copy-start(bf16[256,4096]{0,1:T(8,128)(2,1)} %copy.32) | copy-start | bytes 6291460
  102.0 8.3 %copy-start.8 = (bf16[32,32,8,128]{3,2,1,0:T(8,128)(2,1)S(1)}, bf16[32,32,8,128]{3,2,1,0:T(8,128)(2,1)}, u32[]{:S(2)}) copy-start(bf16[32,32,8,128]{3,2,1,0:T(8,128)(2,1)} %fusion.51) | copy-start | bytes 6291460
  111.8 1.8 copy-start.2
  113.7 2.1 copy-start
  113.7 8.6 %slice-start = ((s8[8388608]{0:T(1024)(128)(4,1)}), s8[4194304]{0:T(1024)(128)(4,1)S(1)}, s32[]{:S(2)}) async-start(s8[8388608]{0:T(1024)(128)(4,1)} %bitcast.133), calls=%async_computation.7 | async-start | bytes 8388608
  115.8 6.5 %slice-start.1 = ((s8[8388608]{0:T(1024)(128)(4,1)}), s8[4194304]{0:T(1024)(128)(4,1)S(1)}, s32[]{:S(2)}) async-start(s8[8388608]{0:T(1024)(128)(4,1)} %bitcast.133), calls=%async_computation.8 | async-start | bytes 8388608
  115.8 6.5 %copy-start.7 = (bf16[32,128,256]{2,1,0:T(8,128)(2,1)S(1)}, bf16[32,128,256]{2,1,0:T(8,128)(2,1)}, u32[]{:S(2)}) copy-start(bf16[32,128,256]{2,1,0:T(8,128)(2,1)} %fusion.41) | copy-start | bytes 6291460
  125.7 56.7 %reduce-scatter.4.cloned.1.call-start = ((), (), s32[]{:S(2)}) async-start(), calls=%async_computation.3 | async-start | bytes 1310720 | tf_op jit(solution)/shard_map/reduce_scatter | solution.py:67
  138.1 80.5 %reduce-scatter.6.cloned.1.call-start = ((), (), s32[]{:S(2)}) async-start(), calls=%async_computation.4 | async-start | bytes 1310720 | tf_op jit(solution)/shard_map/reduce_scatter | solution.py:69
  147.9 87.5 %all-reduce.3.cloned.1.call-start = ((), (), s32[]{:S(2)}) async-start(), calls=%async_computation.6 | async-start | bytes 524288 | tf_op jit(solution)/shard_map/psum | solution.py:76
Sparse Core Ops, SparseCore 0:
  125.9 28.4 reduce-scatter.7
  156.7 25.7 reduce-scatter.3
  184.8 26.6 reduce-scatter.5
  213.6 21.7 all-reduce.2
where the time goes:
time: 246 us; the launch traced here: 245 us
  blocking collectives  82.2 us (33%)
  matrix products  76.1 us (31%)
  waiting for transfers between devices  49.1 us (20%)
  between operations  17 us (7%)
  local copies, waits for them, and re-layouts  11.9 us (5%)
  other arithmetic  8.67 us (4%)
    psum x1, blocking collectives, local(): lax.psum((loss_part, count_local / lax.axis_size('mp')), ('dp', 'mp'))  32.6 us
    reduce_scatter x1, waiting for transfers between devices, local(): out_sum = lax.psum_scatter(out_part, 'mp', scatter_dimension=2, tiled=True)  28.1 us
    all_gather x1, blocking collectives, local(): lax.all_gather(memory, 'mp', axis=2, tiled=True)  17.6 us
    all_gather x1, blocking collectives, local(): lax.all_gather(states[0], 'mp', axis=2, tiled=True)  16.6 us
    all_gather x1, blocking collectives, local(): lax.all_gather(targets[0], 'mp', axis=2, tiled=True)  15.5 us
    psum x1, waiting for transfers between devices, local(): grad_mem = lax.psum(grad_m, 'phase')  14.5 us
    another operation x3, local copies, waits for them, and re-layouts  9.89 us
    sub x1, matrix products, local(): probs = jax.nn.softmax(scores, axis=-1)  7.56 us
  transfers between devices with their start and end apart: 4, of which 3 were waited for; matrix products, arithmetic and copies ran while one was open for 11% of the time, Pallas kernels for 0%

commit v1 on v0

v1 whole, which is shorter than its diff:
```python
import functools

import jax
import jax.numpy as jnp
from jax import lax
from jax.experimental import pallas as pl
from jax.experimental.pallas import tpu as pltpu
from jax.sharding import PartitionSpec as P

HEAD = 128
EXCLUDED = -1e30
F32 = jnp.float32
BF16 = jnp.bfloat16
VMEM_LIMIT = 60 * 1024 * 1024


def block_width(inner):
    for width in (512, 256):
        if inner % width == 0:
            return width
    return HEAD


def nt(a, b):
    return lax.dot_general(a, b, (((1,), (1,)), ((), ())), preferred_element_type=F32)


def nn(a, b):
    return lax.dot_general(a, b, (((1,), (0,)), ((), ())), preferred_element_type=F32)


def tn(a, b):
    return lax.dot_general(a, b, (((0,), (0,)), ((), ())), preferred_element_type=F32)


def row_copies(idx, hbm, buf, sem, pieces, chunk, width, g):
    return [
        pltpu.make_async_copy(
            hbm.at[pl.ds(pl.multiple_of(idx[s] * chunk, chunk), chunk), pl.ds(pl.multiple_of(g * width, width), width)],
            buf.at[g, pl.ds(s * chunk, chunk), :],
            sem.at[g, s],
        )
        for s in range(pieces)
    ]


def column_copies(idx, hbm, buf, sem, pieces, chunk, width, g):
    return [
        pltpu.make_async_copy(
            hbm.at[pl.ds(pl.multiple_of(g * width, width), width), pl.ds(pl.multiple_of(idx[s] * chunk, chunk), chunk)],
            buf.at[g, :, pl.ds(s * chunk, chunk)],
            sem.at[g, s],
        )
        for s in range(pieces)
    ]


def start_all(blocks, makers):
    @pl.loop(0, blocks)
    def _(g):
        for make in makers:
            for copy in make(g):
                copy.start()


def wait_all(copies):
    for copy in copies:
        copy.wait()


def kv_kernel(pieces, idx, *refs):
    parts, (wk, wv, k_out, v_out, cat, kbuf, vbuf, ksem, vsem) = refs[:pieces], refs[pieces:]
    g, blocks = pl.program_id(0), pl.num_programs(0)
    chunk, width = parts[0].shape[1], k_out.shape[1]
    make_k = functools.partial(row_copies, idx, wk, kbuf, ksem, pieces, chunk, width)
    make_v = functools.partial(row_copies, idx, wv, vbuf, vsem, pieces, chunk, width)

    @pl.when(g == 0)
    def _():
        start_all(blocks, (make_k, make_v))
        for s in range(pieces):
            cat[:, s * chunk : (s + 1) * chunk] = parts[s][...]

    wait_all(make_k(g))
    k_out[...] = nn(cat[...], kbuf[g]).astype(BF16)
    wait_all(make_v(g))
    v_out[...] = nn(cat[...], vbuf[g]).astype(BF16)


def forward_kernel(pieces, idx, *refs):
    parts = refs[:pieces]
    src, tgt, k, v, wq, wo, q_out, p_out = refs[pieces : pieces + 8]
    outs = refs[pieces + 8 : 2 * pieces + 8]
    cat, bias, acc, qbuf, obuf, qsem, osem = refs[2 * pieces + 8 :]
    g, blocks = pl.program_id(0), pl.num_programs(0)
    chunk, width = parts[0].shape[1], q_out.shape[1]
    make_q = functools.partial(row_copies, idx, wq, qbuf, qsem, pieces, chunk, width)
    make_o = functools.partial(column_copies, idx, wo, obuf, osem, pieces, chunk, width)

    @pl.when(g == 0)
    def _():
        start_all(blocks, (make_q, make_o))
        for s in range(pieces):
            cat[:, s * chunk : (s + 1) * chunk] = parts[s][...]
        bias[...] = jnp.where(src[...] == tgt[...], 0.0, EXCLUDED).astype(F32)
        acc[...] = jnp.zeros_like(acc)

    wait_all(make_q(g))
    q = nn(cat[...], qbuf[g]).astype(BF16)
    q_out[...] = q
    attended = []
    for h in range(width // HEAD):
        at = slice(h * HEAD, (h + 1) * HEAD)
        scores = nt(k[:, at], q[:, at]) + bias[...]
        weights = jnp.exp(scores - jnp.max(scores, axis=0, keepdims=True))
        probs = weights * (1.0 / jnp.sum(weights, axis=0, keepdims=True))
        p_out[h] = probs
        attended.append(tn(probs.astype(BF16), v[:, at]).astype(BF16))
    wait_all(make_o(g))
    acc[...] += nn(jnp.concatenate(attended, axis=1), obuf[g])

    @pl.when(g == blocks - 1)
    def _():
        for s in range(pieces):
            outs[s][...] = acc[:, s * chunk : (s + 1) * chunk].astype(outs[s].dtype)


def backward_kernel(pieces, idx, count, *refs):
    parts = refs[:pieces]
    q, k, v, p, wq, wo, dk_out, dv_out = refs[pieces : pieces + 8]
    outs = refs[pieces + 8 : 2 * pieces + 8]
    cat, acc, qbuf, obuf, qsem, osem = refs[2 * pieces + 8 :]
    g, blocks = pl.program_id(0), pl.num_programs(0)
    chunk, width = parts[0].shape[1], q.shape[1]
    make_q = functools.partial(row_copies, idx, wq, qbuf, qsem, pieces, chunk, width)
    make_o = functools.partial(column_copies, idx, wo, obuf, osem, pieces, chunk, width)

    @pl.when(g == 0)
    def _():
        start_all(blocks, (make_o, make_q))
        valid = lax.broadcasted_iota(jnp.int32, parts[0].shape, 0) < count[0]
        for s in range(pieces):
            cat[:, s * chunk : (s + 1) * chunk] = jnp.where(valid, parts[s][...], jnp.zeros_like(parts[s]))
        acc[...] = jnp.zeros_like(acc)

    wait_all(make_o(g))
    grad_att = nt(cat[...], obuf[g]).astype(BF16)
    grad_q = []
    for h in range(width // HEAD):
        at = slice(h * HEAD, (h + 1) * HEAD)
        probs = p[h]
        grad_prob = nt(v[:, at], grad_att[:, at])
        inner = jnp.sum(probs * grad_prob, axis=0, keepdims=True)
        grad_score = (probs * (grad_prob - inner)).astype(BF16)
        grad_q.append(tn(grad_score, k[:, at]).astype(BF16))
        dk_out[:, at] = nn(grad_score, q[:, at]).astype(BF16)
        dv_out[:, at] = nn(probs.astype(BF16), grad_att[:, at]).astype(BF16)
    wait_all(make_q(g))
    acc[...] += nt(jnp.concatenate(grad_q, axis=1), qbuf[g])

    @pl.when(g == blocks - 1)
    def _():
        for s in range(pieces):
            outs[s][...] = acc[:, s * chunk : (s + 1) * chunk].astype(outs[s].dtype)


def memory_kernel(which, chunk, idx, dk, dv, wk, wv, *refs):
    outs, (kbuf, vbuf, ksem, vsem) = refs[: len(which)], refs[len(which) :]

    def copies(i):
        rows = pl.ds(pl.multiple_of(idx[which[i]] * chunk, chunk), chunk)
        return (
            pltpu.make_async_copy(wk.at[rows, :], kbuf.at[i], ksem.at[i]),
            pltpu.make_async_copy(wv.at[rows, :], vbuf.at[i], vsem.at[i]),
        )

    for i in range(len(which)):
        for copy in copies(i):
            copy.start()
    for i in range(len(which)):
        wait_all(copies(i))
        outs[i][...] = (nt(dk[...], kbuf[i]) + nt(dv[...], vbuf[i])).astype(outs[i].dtype)


def whole(shape):
    return pl.BlockSpec(shape, lambda *_: (0,) * len(shape))


ANY = pl.BlockSpec(memory_space=pl.ANY)
SMEM = pl.BlockSpec(memory_space=pltpu.SMEM)


def params():
    return pltpu.CompilerParams(vmem_limit_bytes=VMEM_LIMIT)


def cost(flops, bytes_accessed, transcendentals=0):
    return pl.CostEstimate(flops=flops, bytes_accessed=bytes_accessed, transcendentals=transcendentals)


def piece_types(rows, chunk, pieces, first=0):
    return [jax.ShapeDtypeStruct((rows, chunk), F32 if s == 0 else BF16) for s in range(first, pieces)]


def project_kv(idx, parts, wk, wv):
    pieces, (rows, chunk), (features, inner) = len(parts), parts[0].shape, wk.shape
    width = block_width(inner)
    blocks = inner // width
    column = pl.BlockSpec((rows, width), lambda g: (0, g))
    return pl.pallas_call(
        functools.partial(kv_kernel, pieces),
        grid=(blocks,),
        in_specs=[SMEM] + [whole((rows, chunk))] * pieces + [ANY, ANY],
        out_specs=[column, column],
        out_shape=[jax.ShapeDtypeStruct((rows, inner), BF16)] * 2,
        scratch_shapes=[
            pltpu.VMEM((rows, features), BF16),
            pltpu.VMEM((blocks, features, width), BF16),
            pltpu.VMEM((blocks, features, width), BF16),
            pltpu.SemaphoreType.DMA((blocks, pieces)),
            pltpu.SemaphoreType.DMA((blocks, pieces)),
        ],
        compiler_params=params(),
        cost_estimate=cost(4 * rows * features * inner, 4 * features * inner),
        name="project_kv",
    )(idx, *parts, wk, wv)


def attend(idx, parts, src, tgt, k, v, wq, wo):
    pieces, (rows, chunk), (features, inner) = len(parts), parts[0].shape, wq.shape
    src_len = k.shape[0]
    width = block_width(inner)
    blocks, heads = inner // width, width // HEAD
    key_block = pl.BlockSpec((src_len, width), lambda g: (0, g))
    query_block = pl.BlockSpec((rows, width), lambda g: (0, g))
    prob_block = pl.BlockSpec((heads, src_len, rows), lambda g: (g, 0, 0))
    return pl.pallas_call(
        functools.partial(forward_kernel, pieces),
        grid=(blocks,),
        in_specs=[SMEM]
        + [whole((rows, chunk))] * pieces
        + [whole((src_len, 1)), whole((1, rows)), key_block, key_block, ANY, ANY],
        out_specs=[query_block, prob_block] + [whole((rows, chunk))] * pieces,
        out_shape=[
            jax.ShapeDtypeStruct((rows, inner), BF16),
            jax.ShapeDtypeStruct((inner // HEAD, src_len, rows), F32),
        ]
        + piece_types(rows, chunk, pieces),
        scratch_shapes=[
            pltpu.VMEM((rows, features), BF16),
            pltpu.VMEM((src_len, rows), F32),
            pltpu.VMEM((rows, features), F32),
            pltpu.VMEM((blocks, features, width), BF16),
            pltpu.VMEM((blocks, width, features), BF16),
            pltpu.SemaphoreType.DMA((blocks, pieces)),
            pltpu.SemaphoreType.DMA((blocks, pieces)),
        ],
        compiler_params=params(),
        cost_estimate=cost(6 * rows * features * inner, 8 * features * inner),
        name="attend",
    )(idx, *parts, src, tgt, k, v, wq, wo)


def attend_backward(idx, count, parts, q, k, v, p, wq, wo):
    pieces, (rows, chunk), (features, inner) = len(parts), parts[0].shape, wq.shape
    src_len = k.shape[0]
    width = block_width(inner)
    blocks, heads = inner // width, width // HEAD
    key_block = pl.BlockSpec((src_len, width), lambda g: (0, g))
    query_block = pl.BlockSpec((rows, width), lambda g: (0, g))
    prob_block = pl.BlockSpec((heads, src_len, rows), lambda g: (g, 0, 0))
    return pl.pallas_call(
        functools.partial(backward_kernel, pieces),
        grid=(blocks,),
        in_specs=[SMEM, SMEM]
        + [whole((rows, chunk))] * pieces
        + [query_block, key_block, key_block, prob_block, ANY, ANY],
        out_specs=[key_block, key_block] + [whole((rows, chunk))] * pieces,
        out_shape=[jax.ShapeDtypeStruct((src_len, inner), BF16)] * 2 + piece_types(rows, chunk, pieces),
        scratch_shapes=[
            pltpu.VMEM((rows, features), BF16),
            pltpu.VMEM((rows, features), F32),
            pltpu.VMEM((blocks, features, width), BF16),
            pltpu.VMEM((blocks, width, features), BF16),
            pltpu.SemaphoreType.DMA((blocks, pieces)),
            pltpu.SemaphoreType.DMA((blocks, pieces)),
        ],
        compiler_params=params(),
        cost_estimate=cost(8 * rows * features * inner, 8 * features * inner),
        name="attend_backward",
    )(idx, count, *parts, q, k, v, p, wq, wo)


def memory_grads(idx, which, chunk, dk, dv, wk, wv):
    rows, inner = dk.shape
    full = pl.BlockSpec(memory_space=pltpu.VMEM)
    return pl.pallas_call(
        functools.partial(memory_kernel, which, chunk),
        in_specs=[SMEM, full, full, ANY, ANY],
        out_specs=[full] * len(which),
        out_shape=[jax.ShapeDtypeStruct((rows, chunk), F32 if s == 0 else BF16) for s in which],
        scratch_shapes=[
            pltpu.VMEM((len(which), chunk, inner), BF16),
            pltpu.VMEM((len(which), chunk, inner), BF16),
            pltpu.SemaphoreType.DMA((len(which),)),
            pltpu.SemaphoreType.DMA((len(which),)),
        ],
        compiler_params=params(),
        cost_estimate=cost(4 * rows * chunk * len(which) * inner, 4 * chunk * len(which) * inner),
        name="memory_grads",
    )(idx, dk, dv, wk, wv)


def swap(x, axis, step):
    size = lax.axis_size(axis)
    return lax.ppermute(x, axis, [(i, i ^ step) for i in range(size)])


def butterfly(x, axis):
    step = 1
    while step < lax.axis_size(axis):
        x = x + swap(x, axis, step)
        step *= 2
    return x


def local(direct, memory, states, targets, w_query, w_key, w_value, w_out, src_ids, tgt_ids, counts):
    n = lax.axis_size("mp")
    mem, state, target = memory[0], states[0, 0], targets[0, 0]
    wq, wk, wv, wo = w_query[0], w_key[0], w_value[0], w_out[0]
    chunk = mem.shape[1]
    valid = jnp.arange(target.shape[0])[:, None] < counts[0]
    grad_own = jnp.where(valid, target, jnp.zeros_like(target)).astype(F32)
    src, tgt = src_ids.reshape(-1, 1), tgt_ids.reshape(1, -1)
    if direct:
        idx = lax.axis_index("mp") ^ jnp.arange(n, dtype=jnp.int32)

        def gather(x):
            return [x] + [swap(x, "mp", s) for s in range(1, n)]

        def scatter(parts):
            total = parts[0]
            for s in range(1, n):
                total = total + swap(parts[s], "mp", s).astype(F32)
            return total
    else:
        idx = jnp.zeros((1,), jnp.int32)
        chunk = chunk * n

        def gather(x):
            return [lax.all_gather(x, "mp", axis=1, tiled=True)]

        def scatter(parts):
            return lax.psum_scatter(parts[0], "mp", scatter_dimension=1, tiled=True)

    pieces = n if direct else 1
    mem_parts, state_parts, target_parts = gather(mem), gather(state), gather(target)
    k, v = project_kv(idx, mem_parts, wk, wv)
    q, p, *out_parts = attend(idx, state_parts, src, tgt, k, v, wq, wo)
    out_low = scatter(out_parts).astype(BF16)
    dk, dv, *grad_x_parts = attend_backward(idx, counts, target_parts, q, k, v, p, wq, wo)
    grad_x = scatter(grad_x_parts)
    grad_m_parts = memory_grads(idx, tuple(range(pieces)), chunk, dk, dv, wk, wv)
    grad_m = scatter(grad_m_parts)

    loss_part = jnp.sum(out_low.astype(F32) * grad_own)
    count_part = counts[0].astype(F32) / n
    if direct:
        sums = butterfly(butterfly(jnp.stack([loss_part, count_part]), "mp"), "dp")
        loss_total, count_total = sums[0], sums[1]
        grad_m = lax.reduce_precision(grad_m, 8, 7)
        grad_m = grad_m + swap(grad_m.astype(BF16), "phase", 1).astype(F32)
    else:
        loss_total, count_total = lax.psum((loss_part, count_part), ("dp", "mp"))
        grad_m = lax.psum(grad_m, "phase")
    loss = (loss_total / count_total).reshape(1)
    states_grad = (grad_x / count_total).astype(BF16)
    memory_grad = (grad_m / count_total).astype(BF16)
    return out_low[None, None], loss, states_grad[None, None], memory_grad[None]


def power_of_two(size):
    return size & (size - 1) == 0


def solution(mesh):
    sizes = mesh.shape
    placed = (
        P("dp", None, "mp"),
        P("phase", "dp", None, "mp"),
        P("phase", "dp", None, "mp"),
        P("phase", None, "mp"),
        P("phase", None, "mp"),
        P("phase", None, "mp"),
        P("phase", "mp", None),
        P("dp", None),
        P("dp", None),
        P("dp"),
    )
    direct = 1 < sizes["mp"] <= 4 and power_of_two(sizes["mp"]) and power_of_two(sizes["dp"]) and sizes["phase"] == 2
    return jax.shard_map(
        functools.partial(local, direct),
        mesh=mesh,
        in_specs=placed,
        out_specs=(
            P("phase", "dp", None, "mp"),
            P("phase"),
            P("phase", "dp", None, "mp"),
            P("dp", None, "mp"),
        ),
        check_vma=False,
    )
```

time: 246 us -> 141 us (0.57)
  blocking collectives: 82.2 us -> 0 us
  matrix products: 76.1 us -> 0 us
  Pallas kernels: 0 us -> 71 us
  starting transfers between devices: 0.38 us -> 36.4 us
  waiting for transfers between devices: 49.1 us -> 16.7 us
  between operations: 17 us -> 3.89 us
  local copies, waits for them, and re-layouts: 11.9 us -> 4.08 us
    pallas_call x0 -> x4, Pallas kernels: none -> 71 us  [the longest x1 24.4 us: attend_backward(): pl.pallas_call(functools.partial(backward_kernel, pieces), grid=(blocks,)...]
    dot_general x13 -> x0, matrix products: 68.5 us -> none  [the longest x1 7.11 us: local(): jnp.einsum('btd,kd->btk', grad_out, wo, preferred_element_type=jnp.float32)]
    all_gather x3 -> x0, blocking collectives: 49.6 us -> none  [the longest x1 17.6 us: local(): lax.all_gather(memory, 'mp', axis=2, tiled=True)]
    ppermute x0 -> x23, starting transfers between devices: none -> 36.4 us  [swap(): return lax.ppermute(x, axis, [(i, i ^ step) for i in range(size)])]
    reduce_scatter x3 -> x0, waiting for transfers between devices: 34.5 us -> none  [the longest x1 28.1 us: local(): out_sum = lax.psum_scatter(out_part, 'mp', scatter_dimension=2, tiled=True)]
    psum x1 -> x0, blocking collectives: 32.6 us -> none  [local(): lax.psum((loss_part, count_local / lax.axis_size('mp')), ('dp', 'mp'))]
    ppermute x0 -> x23, waiting for transfers between devices: none -> 16.7 us  [swap(): return lax.ppermute(x, axis, [(i, i ^ step) for i in range(size)])]
    psum x1 -> x0, waiting for transfers between devices: 14.5 us -> none  [local(): grad_mem = lax.psum(grad_m, 'phase')]
  transfers between devices with their start and end apart: 4 -> 23, of which waited for: 3 -> 7; matrix products, arithmetic and copies ran while one was open for 11% -> 6% of each run, Pallas kernels for 0% -> 50%
where the time goes in v1:
time: 141 us
  Pallas kernels  71 us (50%)
  starting transfers between devices  36.4 us (26%)
  waiting for transfers between devices  16.7 us (12%)
  other arithmetic  8.62 us (6%)
  local copies, waits for them, and re-layouts  4.08 us (3%)
  between operations  3.89 us (3%)
    ppermute x23, starting transfers between devices, swap(): return lax.ppermute(x, axis, [(i, i ^ step) for i in range(size)])  36.4 us
    pallas_call x1, Pallas kernels, attend_backward(): pl.pallas_call(functools.partial(backward_kernel, pieces), grid=(blocks,)...  24.4 us
    pallas_call x1, Pallas kernels, attend(): pl.pallas_call(functools.partial(forward_kernel, pieces), grid=(blocks,),...  20.7 us
    ppermute x23, waiting for transfers between devices, swap(): return lax.ppermute(x, axis, [(i, i ^ step) for i in range(size)])  16.7 us
    pallas_call x1, Pallas kernels, memory_grads(): pl.pallas_call(functools.partial(memory_kernel, which, chunk), in_specs=[...  14.6 us
    pallas_call x1, Pallas kernels, project_kv(): pl.pallas_call(functools.partial(kv_kernel, pieces), grid=(blocks,), in_s...  11.3 us
  transfers between devices with their start and end apart: 23, of which 7 were waited for; matrix products, arithmetic and copies ran while one was open for 6% of the time, Pallas kernels for 50%

profile of v1, /device:TPU:0, one launch (start us, length us, event | category | flops | bytes accessed | tf_op | source)
XLA Modules:
  0.0 140.8 jit_solution(763490298164968801)
XLA Ops:
  0.6 5.1 %collective-permute-start.5 = (bf16[256,256]{1,0:T(8,128)(2,1)}, bf16[256,256]{1,0:T(8,128)(2,1)S(1)}, u32[]{:S(2)}, u32[]{:S(2)}) collective-permute-start(bf16[256,256]{1,0:T(8,128)(2,1)} %bitcast.34), channel_id=1, source_target_pairs={{0,3},{1,2},{2,1},{3,0},{4,7},{5,6},{6,5},{7,4},{8,11},{9,10},{10,... | collective-permute-start | bytes 393224 | tf_op jit(solution)/shard_map/ppermute | solution.py:316
  6.4 3.7 %collective-permute-start.2 = (bf16[256,256]{1,0:T(8,128)(2,1)}, bf16[256,256]{1,0:T(8,128)(2,1)S(1)}, u32[]{:S(2)}, u32[]{:S(2)}) collective-permute-start(bf16[256,256]{1,0:T(8,128)(2,1)} %bitcast.40), channel_id=1, source_target_pairs={{0,3},{1,2},{2,1},{3,0},{4,7},{5,6},{6,5},{7,4},{8,11},{9,10},{10,... | collective-permute-start | bytes 393224 | tf_op jit(solution)/shard_map/ppermute | solution.py:316
  11.4 1.5 %copy.14.refs_4_ = s32[256,1]{1,0:T(8,128)} copy(s32[256,1]{0,1:T(1,128)} %bitcast.39) | data formatting | bytes 2048 | tf_op jit(solution)/shard_map/reshape | solution.py:334
  12.9 3.7 %collective-permute-start = (bf16[256,256]{1,0:T(8,128)(2,1)}, bf16[256,256]{1,0:T(8,128)(2,1)S(1)}, u32[]{:S(2)}, u32[]{:S(2)}) collective-permute-start(bf16[256,256]{1,0:T(8,128)(2,1)} %bitcast.42), channel_id=1, source_target_pairs={{0,1},{1,0},{2,3},{3,2},{4,5},{5,4},{6,7},{7,6},{8,9},{9,8},{10,11... | collective-permute-start | bytes 393224 | tf_op jit(solution)/shard_map/ppermute | solution.py:316
  16.6 7.0 %collective-permute-done.4.refs_2_ = bf16[256,256]{1,0:T(8,128)(2,1)S(1)} collective-permute-done((bf16[256,256]{1,0:T(8,128)(2,1)}, bf16[256,256]{1,0:T(8,128)(2,1)S(1)}, u32[]{:S(2)}, u32[]{:S(2)}) %collective-permute-start.4) | collective-permute-done | bytes 131104 | tf_op jit(solution)/shard_map/ppermute | solution.py:316
  23.6 2.7 %collective-permute-start.15 = (bf16[256,256]{1,0:T(8,128)(2,1)}, bf16[256,256]{1,0:T(8,128)(2,1)S(1)}, u32[]{:S(2)}, u32[]{:S(2)}) collective-permute-start(bf16[256,256]{1,0:T(8,128)(2,1)} %bitcast.30), channel_id=1, source_target_pairs={{0,3},{1,2},{2,1},{3,0},{4,7},{5,6},{6,5},{7,4},{8,11},{9,10},{10,... | collective-permute-start | bytes 393224 | tf_op jit(solution)/shard_map/ppermute | solution.py:316
  26.9 11.3 %project_kv.1 = (bf16[256,4096]{1,0:T(8,128)(2,1)}, bf16[256,4096]{1,0:T(8,128)(2,1)}) custom-call(s32[4]{0:T(128)} %iota_xor_fusion.idx, bf16[256,256]{1,0:T(8,128)(2,1)} %bitcast.37, bf16[256,256]{1,0:T(8,128)(2,1)} %copy-done.9, bf16[256,256]{1,0:T(8,128)(2,1)} %copy-done.7, bf16[256,256]{1,0:T(8,128)(2,1)} %copy-done.6, bf16[1024,4096]{1,0:T(8,128)(2,1)} %bitcast.22, ...), custom_call_target="tpu_custom_call" | custom-call | flops 4294967296 | bytes 16777216 | tf_op jit(solution)/shard_map/project_kv/pallas_call | solution.py:210
  38.3 1.2 collective-permute-start.13
  40.2 20.7 %attend.1 = (bf16[256,4096]{1,0:T(8,128)(2,1)}, f32[32,256,256]{2,1,0:T(8,128)}, f32[256,256]{1,0:T(8,128)}, bf16[256,256]{1,0:T(8,128)(2,1)}, bf16[256,256]{1,0:T(8,128)(2,1)}, /*index=5*/bf16[256,256]{1,0:T(8,128)(2,1)}) custom-call(s32[4]{0:T(128)} %iota_xor_fusion.idx, bf16[256,256]{1,0:T(8,128)(2,1)} %bitcast.43, bf16[256,256]{1,0:T(8,128)(2,1)} %copy-done.13, ...), custom_call_target="tpu_custom_call" | custom-call | flops 6442450944 | bytes 33554432 | tf_op jit(solution)/shard_map/attend/pallas_call | solution.py:237
  61.9 2.3 %collective-permute-start.7 = (bf16[256,256]{1,0:T(8,128)(2,1)}, bf16[256,256]{1,0:T(8,128)(2,1)S(1)}, u32[]{:S(2)}, u32[]{:S(2)}) collective-permute-start(bf16[256,256]{1,0:T(8,128)(2,1)} %get-tuple-element.26), channel_id=1, source_target_pairs={{0,2},{1,3},{2,0},{3,1},{4,6},{5,7},{6,4},{7,5},{8,10},{9,11},{10,... | collective-permute-start | bytes 393224 | tf_op jit(solution)/shard_map/ppermute | solution.py:316
  66.1 24.4 %attend_backward.1 = (bf16[256,4096]{1,0:T(8,128)(2,1)}, bf16[256,4096]{1,0:T(8,128)(2,1)}, f32[256,256]{1,0:T(8,128)}, bf16[256,256]{1,0:T(8,128)(2,1)}, bf16[2...) custom-call(s32[4]{0:T(128)} %iota_xor_fusion.idx, s32[1]{0:T(128)} %copy.15.count, bf16[256,256]{1,0:T(8,128)(2,1)} %bitcast.32, ...), custom_call_target="tpu_custom_call" | custom-call | flops 8589934592 | bytes 33554432 | tf_op jit(solution)/shard_map/attend_backward/pallas_call | solution.py:272
  90.6 3.2 %collective-permute-start.17 = (bf16[256,256]{1,0:T(8,128)(2,1)}, bf16[256,256]{1,0:T(8,128)(2,1)S(1)}, u32[]{:S(2)}, u32[]{:S(2)}) collective-permute-start(bf16[256,256]{1,0:T(8,128)(2,1)} %get-tuple-element.32), channel_id=1, source_target_pairs={{0,2},{1,3},{2,0},{3,1},{4,6},{5,7},{6,4},{7,5},{8,10},{9,11},{10,... | collective-permute-start | bytes 393224 | tf_op jit(solution)/shard_map/ppermute | solution.py:316
  93.8 14.6 %memory_grads.1 = (f32[256,256]{1,0:T(8,128)}, bf16[256,256]{1,0:T(8,128)(2,1)}, bf16[256,256]{1,0:T(8,128)(2,1)}, bf16[256,256]{1,0:T(8,128)(2,1)}) custom-call(s32[4]{0:T(128)} %iota_xor_fusion.idx, bf16[256,4096]{1,0:T(8,128)(2,1)} %get-tuple-element.34.dk, bf16[256,4096]{1,0:T(8,128)(2,1)} %get-tuple-element.35.dv, bf16[1024,4096]{1,0:T(8,128)(2,1)} %bitcast.23, ...), custom_call_target="tpu_custom_call" | custom-call | flops 4294967296 | bytes 16777216 | tf_op jit(solution)/shard_map/memory_grads/pallas_call | solution.py:297
  108.6 1.7 %collective-permute-start.20 = (bf16[256,256]{1,0:T(8,128)(2,1)}, bf16[256,256]{1,0:T(8,128)(2,1)S(1)}, u32[]{:S(2)}, u32[]{:S(2)}) collective-permute-start(bf16[256,256]{1,0:T(8,128)(2,1)} %get-tuple-element.38), channel_id=1, source_target_pairs={{0,2},{1,3},{2,0},{3,1},{4,6},{5,7},{6,4},{7,5},{8,10},{9,11},{10,... | collective-permute-start | bytes 393224 | tf_op jit(solution)/shard_map/ppermute | solution.py:316
  110.2 2.7 %collective-permute-start.21 = (bf16[256,256]{1,0:T(8,128)(2,1)}, bf16[256,256]{1,0:T(8,128)(2,1)S(1)}, u32[]{:S(2)}, u32[]{:S(2)}) collective-permute-start(bf16[256,256]{1,0:T(8,128)(2,1)} %get-tuple-element.39), channel_id=1, source_target_pairs={{0,3},{1,2},{2,1},{3,0},{4,7},{5,6},{6,5},{7,4},{8,11},{9,10},{10,... | collective-permute-start | bytes 393224 | tf_op jit(solution)/shard_map/ppermute | solution.py:316
  112.9 1.3 multiply_reduce_fusion
  116.1 3.5 %collective-permute-done.20 = bf16[256,256]{1,0:T(8,128)(2,1)S(1)} collective-permute-done((bf16[256,256]{1,0:T(8,128)(2,1)}, bf16[256,256]{1,0:T(8,128)(2,1)S(1)}, u32[]{:S(2)}, u32[]{:S(2)}) %collective-permute-start.20) | collective-permute-done | bytes 131104 | tf_op jit(solution)/shard_map/ppermute | solution.py:316
  120.7 1.4 %collective-permute-start.22 = (bf16[256,256]{1,0:T(8,128)(2,1)S(1)}, bf16[256,256]{1,0:T(8,128)(2,1)S(1)}, u32[]{:S(2)}, u32[]{:S(2)}) collective-permute-start(bf16[256,256]{1,0:T(8,128)(2,1)S(1)} %fusion.2), channel_id=1, source_target_pairs={{0,16},{16,0},{1,17},{17,1},{2,18},{18,2},{3,19},{19,3},{4,20},{20... | collective-permute-start | bytes 393224 | tf_op jit(solution)/shard_map/ppermute | solution.py:316
  123.9 3.3 %collective-permute-start.10 = (f32[2]{0:T(128)S(1)}, f32[2]{0:T(128)S(1)}, u32[]{:S(2)}, u32[]{:S(2)}) collective-permute-start(f32[2]{0:T(128)S(1)} %fusion.4), channel_id=1, source_target_pairs={{0,2},{1,3},{2,0},{3,1},{4,6},{5,7},{6,4},{7,5},{8,10},{9,11},{10,... | collective-permute-start | bytes 32 | tf_op jit(solution)/shard_map/ppermute | solution.py:316
  127.2 1.5 %collective-permute-done.10 = f32[2]{0:T(128)S(1)} collective-permute-done((f32[2]{0:T(128)S(1)}, f32[2]{0:T(128)S(1)}, u32[]{:S(2)}, u32[]{:S(2)}) %collective-permute-start.10) | collective-permute-done | bytes 40 | tf_op jit(solution)/shard_map/ppermute | solution.py:316
  130.6 1.5 %collective-permute-start.12 = (f32[2]{0:T(128)S(1)}, f32[2]{0:T(128)S(1)}, u32[]{:S(2)}, u32[]{:S(2)}) collective-permute-start(f32[2]{0:T(128)S(1)} %add.47), channel_id=1, source_target_pairs={{0,8},{4,12},{8,0},{12,4},{1,9},{5,13},{9,1},{13,5},{2,10},{6,14},... | collective-permute-start | bytes 32 | tf_op jit(solution)/shard_map/ppermute | solution.py:316
  132.2 2.0 %collective-permute-done.12 = f32[2]{0:T(128)S(1)} collective-permute-done((f32[2]{0:T(128)S(1)}, f32[2]{0:T(128)S(1)}, u32[]{:S(2)}, u32[]{:S(2)}) %collective-permute-start.12) | collective-permute-done | bytes 40 | tf_op jit(solution)/shard_map/ppermute | solution.py:316
  136.1 1.3 fusion.1
  137.4 2.3 %fusion = bf16[1,256,256]{2,1,0:T(8,128)(2,1)} fusion(f32[]{:T(128)} %bitcast.13, bf16[256,256]{1,0:T(8,128)(2,1)S(1)} %collective-permute-done.22, bf16[256,256]{1,0:T(8,128)(2,1)S(1)} %collective-permute-done.21, bf16[256,256]{1,0:T(8,128)(2,1)S(1)} %collective-permute-done.20, f32[256,256]{1,0:T(8,128)} %get-tuple-element.36, ...), kind=kLoop, calls=%fused_computation.5 | loop fusion | flops 720896 | bytes 917508 | tf_op jit(solution)/shard_map/broadcast_in_dim | solution.py:379
  (67 shorter events, 12.8 us)
Async XLA Ops:
  0.6 12.3 %collective-permute-start.5 = (bf16[256,256]{1,0:T(8,128)(2,1)}, bf16[256,256]{1,0:T(8,128)(2,1)S(1)}, u32[]{:S(2)}, u32[]{:S(2)}) collective-permute-start(bf16[256,256]{1,0:T(8,128)(2,1)} %bitcast.34), channel_id=1, source_target_pairs={{0,3},{1,2},{2,1},{3,0},{4,7},{5,6},{6,5},{7,4},{8,11},{9,10},{10,... | collective-permute-start | bytes 393224 | tf_op jit(solution)/shard_map/ppermute | solution.py:316
  5.8 17.9 %collective-permute-start.4 = (bf16[256,256]{1,0:T(8,128)(2,1)}, bf16[256,256]{1,0:T(8,128)(2,1)S(1)}, u32[]{:S(2)}, u32[]{:S(2)}) collective-permute-start(bf16[256,256]{1,0:T(8,128)(2,1)} %bitcast.35), channel_id=1, source_target_pairs={{0,2},{1,3},{2,0},{3,1},{4,6},{5,7},{6,4},{7,5},{8,10},{9,11},{10,... | collective-permute-start | bytes 393224 | tf_op jit(solution)/shard_map/ppermute | solution.py:316
  5.8 20.5 %collective-permute-start.3 = (bf16[256,256]{1,0:T(8,128)(2,1)}, bf16[256,256]{1,0:T(8,128)(2,1)S(1)}, u32[]{:S(2)}, u32[]{:S(2)}) collective-permute-start(bf16[256,256]{1,0:T(8,128)(2,1)} %bitcast.36), channel_id=1, source_target_pairs={{0,1},{1,0},{2,3},{3,2},{4,5},{5,4},{6,7},{7,6},{8,9},{9,8},{10,11... | collective-permute-start | bytes 393224 | tf_op jit(solution)/shard_map/ppermute | solution.py:316
  6.4 31.8 %collective-permute-start.2 = (bf16[256,256]{1,0:T(8,128)(2,1)}, bf16[256,256]{1,0:T(8,128)(2,1)S(1)}, u32[]{:S(2)}, u32[]{:S(2)}) collective-permute-start(bf16[256,256]{1,0:T(8,128)(2,1)} %bitcast.40), channel_id=1, source_target_pairs={{0,3},{1,2},{2,1},{3,0},{4,7},{5,6},{6,5},{7,4},{8,11},{9,10},{10,... | collective-permute-start | bytes 393224 | tf_op jit(solution)/shard_map/ppermute | solution.py:316
  10.2 29.3 %collective-permute-start.1 = (bf16[256,256]{1,0:T(8,128)(2,1)}, bf16[256,256]{1,0:T(8,128)(2,1)S(1)}, u32[]{:S(2)}, u32[]{:S(2)}) collective-permute-start(bf16[256,256]{1,0:T(8,128)(2,1)} %bitcast.41), channel_id=1, source_target_pairs={{0,2},{1,3},{2,0},{3,1},{4,6},{5,7},{6,4},{7,5},{8,10},{9,11},{10,... | collective-permute-start | bytes 393224 | tf_op jit(solution)/shard_map/ppermute | solution.py:316
  12.9 26.6 %collective-permute-start = (bf16[256,256]{1,0:T(8,128)(2,1)}, bf16[256,256]{1,0:T(8,128)(2,1)S(1)}, u32[]{:S(2)}, u32[]{:S(2)}) collective-permute-start(bf16[256,256]{1,0:T(8,128)(2,1)} %bitcast.42), channel_id=1, source_target_pairs={{0,1},{1,0},{2,3},{3,2},{4,5},{5,4},{6,7},{7,6},{8,9},{9,8},{10,11... | collective-permute-start | bytes 393224 | tf_op jit(solution)/shard_map/ppermute | solution.py:316
  23.6 40.6 %collective-permute-start.15 = (bf16[256,256]{1,0:T(8,128)(2,1)}, bf16[256,256]{1,0:T(8,128)(2,1)S(1)}, u32[]{:S(2)}, u32[]{:S(2)}) collective-permute-start(bf16[256,256]{1,0:T(8,128)(2,1)} %bitcast.30), channel_id=1, source_target_pairs={{0,3},{1,2},{2,1},{3,0},{4,7},{5,6},{6,5},{7,4},{8,11},{9,10},{10,... | collective-permute-start | bytes 393224 | tf_op jit(solution)/shard_map/ppermute | solution.py:316
  26.3 39.1 %collective-permute-start.14 = (bf16[256,256]{1,0:T(8,128)(2,1)}, bf16[256,256]{1,0:T(8,128)(2,1)S(1)}, u32[]{:S(2)}, u32[]{:S(2)}) collective-permute-start(bf16[256,256]{1,0:T(8,128)(2,1)} %bitcast.31), channel_id=1, source_target_pairs={{0,2},{1,3},{2,0},{3,1},{4,6},{5,7},{6,4},{7,5},{8,10},{9,11},{10,... | collective-permute-start | bytes 393224 | tf_op jit(solution)/shard_map/ppermute | solution.py:316
  38.3 27.1 %collective-permute-start.13 = (bf16[256,256]{1,0:T(8,128)(2,1)S(1)}, bf16[256,256]{1,0:T(8,128)(2,1)S(1)}, u32[]{:S(2)}, u32[]{:S(2)}) collective-permute-start(bf16[256,256]{1,0:T(8,128)(2,1)S(1)} %bitcast.33), channel_id=1, source_target_pairs={{0,1},{1,0},{2,3},{3,2},{4,5},{5,4},{6,7},{7,6},{8,9},{9,8},{10,11... | collective-permute-start | bytes 393224 | tf_op jit(solution)/shard_map/ppermute | solution.py:316
  60.9 47.5 %collective-permute-start.6 = (bf16[256,256]{1,0:T(8,128)(2,1)}, bf16[256,256]{1,0:T(8,128)(2,1)S(1)}, u32[]{:S(2)}, u32[]{:S(2)}) collective-permute-start(bf16[256,256]{1,0:T(8,128)(2,1)} %get-tuple-element.25), channel_id=1, source_target_pairs={{0,1},{1,0},{2,3},{3,2},{4,5},{5,4},{6,7},{7,6},{8,9},{9,8},{10,11... | collective-permute-start | bytes 393224 | tf_op jit(solution)/shard_map/ppermute | solution.py:316
  61.9 46.7 %collective-permute-start.7 = (bf16[256,256]{1,0:T(8,128)(2,1)}, bf16[256,256]{1,0:T(8,128)(2,1)S(1)}, u32[]{:S(2)}, u32[]{:S(2)}) collective-permute-start(bf16[256,256]{1,0:T(8,128)(2,1)} %get-tuple-element.26), channel_id=1, source_target_pairs={{0,2},{1,3},{2,0},{3,1},{4,6},{5,7},{6,4},{7,5},{8,10},{9,11},{10,... | collective-permute-start | bytes 393224 | tf_op jit(solution)/shard_map/ppermute | solution.py:316
  64.2 46.0 %collective-permute-start.8 = (bf16[256,256]{1,0:T(8,128)(2,1)}, bf16[256,256]{1,0:T(8,128)(2,1)S(1)}, u32[]{:S(2)}, u32[]{:S(2)}) collective-permute-start(bf16[256,256]{1,0:T(8,128)(2,1)} %get-tuple-element.27), channel_id=1, source_target_pairs={{0,3},{1,2},{2,1},{3,0},{4,7},{5,6},{6,5},{7,4},{8,11},{9,10},{10,... | collective-permute-start | bytes 393224 | tf_op jit(solution)/shard_map/ppermute | solution.py:316
  90.5 45.6 %collective-permute-start.16 = (bf16[256,256]{1,0:T(8,128)(2,1)}, bf16[256,256]{1,0:T(8,128)(2,1)S(1)}, u32[]{:S(2)}, u32[]{:S(2)}) collective-permute-start(bf16[256,256]{1,0:T(8,128)(2,1)} %get-tuple-element.31), channel_id=1, source_target_pairs={{0,1},{1,0},{2,3},{3,2},{4,5},{5,4},{6,7},{7,6},{8,9},{9,8},{10,11... | collective-permute-start | bytes 393224 | tf_op jit(solution)/shard_map/ppermute | solution.py:316
  90.6 45.5 %collective-permute-start.17 = (bf16[256,256]{1,0:T(8,128)(2,1)}, bf16[256,256]{1,0:T(8,128)(2,1)S(1)}, u32[]{:S(2)}, u32[]{:S(2)}) collective-permute-start(bf16[256,256]{1,0:T(8,128)(2,1)} %get-tuple-element.32), channel_id=1, source_target_pairs={{0,2},{1,3},{2,0},{3,1},{4,6},{5,7},{6,4},{7,5},{8,10},{9,11},{10,... | collective-permute-start | bytes 393224 | tf_op jit(solution)/shard_map/ppermute | solution.py:316
  93.8 42.3 %copy-start.2 = (f32[256,256]{1,0:T(8,128)S(1)}, f32[256,256]{1,0:T(8,128)}, u32[]{:S(2)}) copy-start(f32[256,256]{1,0:T(8,128)} %get-tuple-element.30) | copy-start | bytes 786436
  108.4 6.8 %collective-permute-start.19 = (bf16[256,256]{1,0:T(8,128)(2,1)}, bf16[256,256]{1,0:T(8,128)(2,1)S(1)}, u32[]{:S(2)}, u32[]{:S(2)}) collective-permute-start(bf16[256,256]{1,0:T(8,128)(2,1)} %get-tuple-element.37), channel_id=1, source_target_pairs={{0,1},{1,0},{2,3},{3,2},{4,5},{5,4},{6,7},{7,6},{8,9},{9,8},{10,11... | collective-permute-start | bytes 393224 | tf_op jit(solution)/shard_map/ppermute | solution.py:316
  108.6 11.1 %collective-permute-start.20 = (bf16[256,256]{1,0:T(8,128)(2,1)}, bf16[256,256]{1,0:T(8,128)(2,1)S(1)}, u32[]{:S(2)}, u32[]{:S(2)}) collective-permute-start(bf16[256,256]{1,0:T(8,128)(2,1)} %get-tuple-element.38), channel_id=1, source_target_pairs={{0,2},{1,3},{2,0},{3,1},{4,6},{5,7},{6,4},{7,5},{8,10},{9,11},{10,... | collective-permute-start | bytes 393224 | tf_op jit(solution)/shard_map/ppermute | solution.py:316
  110.2 9.4 %collective-permute-start.21 = (bf16[256,256]{1,0:T(8,128)(2,1)}, bf16[256,256]{1,0:T(8,128)(2,1)S(1)}, u32[]{:S(2)}, u32[]{:S(2)}) collective-permute-start(bf16[256,256]{1,0:T(8,128)(2,1)} %get-tuple-element.39), channel_id=1, source_target_pairs={{0,3},{1,2},{2,1},{3,0},{4,7},{5,6},{6,5},{7,4},{8,11},{9,10},{10,... | collective-permute-start | bytes 393224 | tf_op jit(solution)/shard_map/ppermute | solution.py:316
  115.3 20.8 %collective-permute-start.18 = (bf16[256,256]{1,0:T(8,128)(2,1)S(1)}, bf16[256,256]{1,0:T(8,128)(2,1)S(1)}, u32[]{:S(2)}, u32[]{:S(2)}) collective-permute-start(bf16[256,256]{1,0:T(8,128)(2,1)S(1)} %copy-done.10), channel_id=1, source_target_pairs={{0,3},{1,2},{2,1},{3,0},{4,7},{5,6},{6,5},{7,4},{8,11},{9,10},{10,... | collective-permute-start | bytes 393224 | tf_op jit(solution)/shard_map/ppermute | solution.py:316
  119.6 3.6 %collective-permute-start.9 = (f32[2]{0:T(128)S(1)}, f32[2]{0:T(128)S(1)}, u32[]{:S(2)}, u32[]{:S(2)}) collective-permute-start(f32[2]{0:T(128)S(1)} %pad_maximum_fusion), channel_id=1, source_target_pairs={{0,1},{1,0},{2,3},{3,2},{4,5},{5,4},{6,7},{7,6},{8,9},{9,8},{10,11... | collective-permute-start | bytes 32 | tf_op jit(solution)/shard_map/ppermute | solution.py:316
  120.7 16.7 %collective-permute-start.22 = (bf16[256,256]{1,0:T(8,128)(2,1)S(1)}, bf16[256,256]{1,0:T(8,128)(2,1)S(1)}, u32[]{:S(2)}, u32[]{:S(2)}) collective-permute-start(bf16[256,256]{1,0:T(8,128)(2,1)S(1)} %fusion.2), channel_id=1, source_target_pairs={{0,16},{16,0},{1,17},{17,1},{2,18},{18,2},{3,19},{19,3},{4,20},{20... | collective-permute-start | bytes 393224 | tf_op jit(solution)/shard_map/ppermute | solution.py:316
  123.9 4.8 %collective-permute-start.10 = (f32[2]{0:T(128)S(1)}, f32[2]{0:T(128)S(1)}, u32[]{:S(2)}, u32[]{:S(2)}) collective-permute-start(f32[2]{0:T(128)S(1)} %fusion.4), channel_id=1, source_target_pairs={{0,2},{1,3},{2,0},{3,1},{4,6},{5,7},{6,4},{7,5},{8,10},{9,11},{10,... | collective-permute-start | bytes 32 | tf_op jit(solution)/shard_map/ppermute | solution.py:316
  129.5 1.2 collective-permute-start.11
  130.6 3.6 %collective-permute-start.12 = (f32[2]{0:T(128)S(1)}, f32[2]{0:T(128)S(1)}, u32[]{:S(2)}, u32[]{:S(2)}) collective-permute-start(f32[2]{0:T(128)S(1)} %add.47), channel_id=1, source_target_pairs={{0,8},{4,12},{8,0},{12,4},{1,9},{5,13},{9,1},{13,5},{2,10},{6,14},... | collective-permute-start | bytes 32 | tf_op jit(solution)/shard_map/ppermute | solution.py:316
  (13 other events, 92.9 us)

commit v2 on v0

v2 whole, which is shorter than its diff:
```python
import functools

import jax
import jax.numpy as jnp
from jax import lax
from jax.experimental import pallas as pl
from jax.experimental.pallas import tpu as pltpu
from jax.sharding import PartitionSpec as P


HEAD = 128
EXCLUDED = -1e30
F32 = jnp.float32
BF16 = jnp.bfloat16


def block_width(inner):
    for width in (512, 256):
        if inner % width == 0:
            return width
    return HEAD


def nt(a, b):
    return lax.dot_general(a, b, (((1,), (1,)), ((), ())), preferred_element_type=F32)


def nn(a, b):
    return lax.dot_general(a, b, (((1,), (0,)), ((), ())), preferred_element_type=F32)


def tn(a, b):
    return lax.dot_general(a, b, (((0,), (0,)), ((), ())), preferred_element_type=F32)


def columns_of(idx, s, chunk):
    return pl.ds(pl.multiple_of(idx[s] * chunk, chunk), chunk)


def join(idx, cat, parts, value=lambda x: x):
    chunk = parts[0].shape[1]
    for s in range(len(parts)):
        cat[:, columns_of(idx, s, chunk)] = value(parts[s][...])


def load_kernel(*refs):
    half = (len(refs) - 1) // 2
    sources, targets, sems = refs[:half], refs[half:-1], refs[-1]
    copies = []
    for i in range(half):
        rows = sources[i].shape[0] // LOAD_PARTS
        for j in range(LOAD_PARTS):
            at = pl.ds(j * rows, rows)
            copies.append(pltpu.make_async_copy(sources[i].at[at, :], targets[i].at[at, :], sems.at[i, j]))
    for copy in copies:
        copy.start()
    for copy in copies:
        copy.wait()


def blocks_of(inner, width, body):
    @pl.loop(0, inner // width)
    def _(g):
        body(pl.ds(pl.multiple_of(g * width, width), width), g)


def kv_kernel(pieces, idx, *refs):
    parts, (wk, wv, k, v, cat) = refs[:pieces], refs[pieces:]
    inner = wk.shape[1]
    join(idx, cat, parts)

    def body(at, g):
        k[:, at] = nn(cat[...], wk[:, at]).astype(BF16)
        v[:, at] = nn(cat[...], wv[:, at]).astype(BF16)

    blocks_of(inner, block_width(inner), body)


def softmax_terms(k, q, bias):
    scores = nt(k, q) + bias
    top = jnp.max(scores, axis=0, keepdims=True)
    weights = jnp.exp(scores - top)
    return weights, top, 1.0 / jnp.sum(weights, axis=0, keepdims=True)


def head_loop(inner, body):
    heads = head_group(inner)

    @pl.loop(0, inner // HEAD // heads)
    def _(i):
        for j in range(heads):
            h = i * heads + j
            body(pl.ds(pl.multiple_of(h * HEAD, HEAD), HEAD), h)


def forward_kernel(pieces, idx, *refs):
    parts = refs[:pieces]
    src, tgt, k, v, wq, wo, q, stats = refs[pieces : pieces + 8]
    outs = refs[pieces + 8 : 2 * pieces + 8]
    cat, bias, o = refs[2 * pieces + 8 :]
    inner = wq.shape[1]
    width = block_width(inner)
    join(idx, cat, parts)
    bias[...] = jnp.where(src[...] == tgt[...], 0.0, EXCLUDED).astype(F32)

    def project(at, g):
        q[:, at] = nn(cat[...], wq[:, at]).astype(BF16)

    blocks_of(inner, width, project)

    def head(at, h):
        weights, top, scale = softmax_terms(k[:, at], q[:, at], bias[...])
        stats[h, 0:1, :] = top
        stats[h, 1:2, :] = scale
        o[:, at] = tn((weights * scale).astype(BF16), v[:, at]).astype(BF16)

    head_loop(inner, head)

    for s in range(pieces):
        outs[s][...] = nn(o[...], wo[:, columns_of(idx, s, parts[0].shape[1])]).astype(outs[s].dtype)


def backward_kernel(pieces, idx, count, *refs):
    parts = refs[:pieces]
    src, tgt, q, k, v, stats, wq, wo, dk, dv = refs[pieces : pieces + 10]
    outs = refs[pieces + 10 : 2 * pieces + 10]
    cat, bias, do, dq = refs[2 * pieces + 10 :]
    inner = wq.shape[1]
    width = block_width(inner)
    valid = lax.broadcasted_iota(jnp.int32, parts[0].shape, 0) < count[0]
    join(idx, cat, parts, lambda x: jnp.where(valid, x, jnp.zeros_like(x)))
    bias[...] = jnp.where(src[...] == tgt[...], 0.0, EXCLUDED).astype(F32)

    def project(at, g):
        do[:, at] = nt(cat[...], wo[at, :]).astype(BF16)

    blocks_of(inner, width, project)

    def head(at, h):
        probs = jnp.exp(nt(k[:, at], q[:, at]) + bias[...] - stats[h, 0:1, :]) * stats[h, 1:2, :]
        grad_prob = nt(v[:, at], do[:, at])
        inner_sum = jnp.sum(probs * grad_prob, axis=0, keepdims=True)
        grad_score = (probs * (grad_prob - inner_sum)).astype(BF16)
        dq[:, at] = tn(grad_score, k[:, at]).astype(BF16)
        dk[:, at] = nn(grad_score, q[:, at]).astype(BF16)
        dv[:, at] = nn(probs.astype(BF16), do[:, at]).astype(BF16)

    head_loop(inner, head)

    for s in range(pieces):
        outs[s][...] = nt(dq[...], wq[columns_of(idx, s, parts[0].shape[1]), :]).astype(outs[s].dtype)


def memory_kernel(pieces, chunk, idx, dk, dv, wk, wv, keep, send, total):
    kept = keep.shape[1]
    mine, other = (pl.ds(pl.multiple_of(idx[pieces + i] * kept, kept), kept) for i in range(2))
    for s in range(pieces):
        rows = columns_of(idx, s, chunk)
        total[s] = nt(dk[...], wk[rows, :]) + nt(dv[...], wv[rows, :])
        keep[s] = total[s, mine, :]
        send[s] = total[s, other, :].astype(BF16)


def tree(values):
    while len(values) > 1:
        values = [values[i] + values[i + 1] for i in range(0, len(values), 2)]
    return values[0]


def add_up(own, arrived):
    total = own[...]
    for part in arrived:
        total = total + part[...].astype(F32)
    return total


def loss_kernel(count, own, *refs):
    arrived, (target, out, part) = refs[:-3], refs[-3:]
    low = add_up(own, arrived).astype(BF16)
    out[...] = low
    grad = jnp.where(lax.broadcasted_iota(jnp.int32, target.shape, 0) < count[0], target[...].astype(F32), 0.0)
    terms = jnp.sum(low.astype(F32) * grad, axis=0, keepdims=True)
    terms = jnp.broadcast_to(jnp.sum(terms, axis=1, keepdims=True), part.shape)
    first = lax.broadcasted_iota(jnp.int32, part.shape, 0) == 0
    part[...] = jnp.where(first, terms, count[0].astype(F32))


def high_low(x):
    high = x.astype(BF16).astype(F32)
    return high, (x - high).astype(BF16).astype(F32)


def join_kernel(pieces, keep, arrived, *refs):
    terms, outs, sums = refs[: -pieces - 1], refs[-pieces - 1 : -1], refs[-1]
    rows, columns = keep.shape[1], keep.shape[2]
    sums[...] = tree([term[...] for term in terms])
    extra = (EXTRA, columns)
    high, low = high_low(jnp.broadcast_to(sums[0:1, 0:1], extra))
    tail = jnp.where(lax.broadcasted_iota(jnp.int32, extra, 0) == 0, high, low).astype(BF16)
    outs[0][...] = keep[0] + arrived[0].astype(F32)
    for s in range(1, pieces):
        outs[s][0:rows, :] = (keep[s] + arrived[s].astype(F32)).astype(BF16)
        outs[s][rows : rows + EXTRA, :] = tail


def final_kernel(pieces, sums, *refs):
    own_m, arrived_m = refs[0], refs[1:pieces]
    own_x, arrived_x = refs[pieces], refs[pieces + 1 : 2 * pieces]
    grad_m, grad_x, loss = refs[2 * pieces :]
    rows = own_m.shape[0]
    count = sums[1:2, 0:1]
    grad_x[...] = (add_up(own_x, arrived_x) / count).astype(BF16)
    total = own_m[...]
    terms = [sum(high_low(sums[0:1, 0:1]))]
    for part in arrived_m:
        total = total + part[0:rows, :].astype(F32)
        tail = part[rows : rows + EXTRA, :].astype(F32)
        terms.append(tail[0:1, 0:1] + tail[1:2, 0:1])
    grad_m[...] = (total / count).astype(BF16)
    loss[...] = jnp.broadcast_to(tree(terms) / count, loss.shape)


EXTRA = 16
TILE = (8, 128)


def memory_whole_kernel(dk, dv, wk, wv, out):
    out[...] = nt(dk[...], wk[...]) + nt(dv[...], wv[...])


LOAD_PARTS = 8
HBM = pl.BlockSpec(memory_space=pltpu.HBM)
SMEM = pl.BlockSpec(memory_space=pltpu.SMEM)
VMEM = pl.BlockSpec(memory_space=pltpu.VMEM)


def head_group(inner):
    return min(8, inner // HEAD)


def params(mib):
    return pltpu.CompilerParams(vmem_limit_bytes=mib * 1024 * 1024)


def cost(flops, bytes_accessed, transcendentals=0):
    return pl.CostEstimate(flops=flops, bytes_accessed=bytes_accessed, transcendentals=transcendentals)


def piece_types(rows, chunk, which):
    return [jax.ShapeDtypeStruct((rows, chunk), F32 if s == 0 else BF16) for s in which]


def dims(parts, weight):
    rows, chunk = parts[0].shape
    features, inner = weight.shape
    return len(parts), rows, chunk, features, inner


def load(*weights):
    return pl.pallas_call(
        load_kernel,
        in_specs=[HBM] * len(weights),
        out_specs=[VMEM] * len(weights),
        out_shape=[pltpu.VMEM(w.shape, w.dtype) for w in weights],
        scratch_shapes=[pltpu.SemaphoreType.DMA((len(weights), LOAD_PARTS))],
        compiler_params=params(12),
        cost_estimate=cost(0, sum(2 * w.size for w in weights)),
        name="load",
    )(*weights)


def plain(kernel, out_types, *operands, smem=0, mib=12):
    return pl.pallas_call(
        kernel,
        in_specs=[SMEM] * smem + [VMEM] * (len(operands) - smem),
        out_specs=[VMEM] * len(out_types),
        out_shape=out_types,
        compiler_params=params(mib),
    )(*operands)


def project_kv(idx, parts, wk, wv):
    pieces, rows, _, features, inner = dims(parts, wk)
    return pl.pallas_call(
        functools.partial(kv_kernel, pieces),
        in_specs=[SMEM] + [VMEM] * (pieces + 2),
        out_specs=[VMEM, VMEM],
        out_shape=[jax.ShapeDtypeStruct((rows, inner), BF16)] * 2,
        scratch_shapes=[
            pltpu.VMEM((rows, features), BF16),
        ],
        compiler_params=params(12),
        cost_estimate=cost(4 * rows * features * inner, 4 * features * inner),
        name="project_kv",
    )(idx, *parts, wk, wv)


def attend(idx, parts, src, tgt, k, v, wq, wo):
    pieces, rows, chunk, features, inner = dims(parts, wq)
    src_len = k.shape[0]
    return pl.pallas_call(
        functools.partial(forward_kernel, pieces),
        in_specs=[SMEM] + [VMEM] * (pieces + 6),
        out_specs=[VMEM] * (2 + pieces),
        out_shape=[
            jax.ShapeDtypeStruct((rows, inner), BF16),
            jax.ShapeDtypeStruct((inner // HEAD, 2, rows), F32),
        ]
        + piece_types(rows, chunk, range(pieces)),
        scratch_shapes=[
            pltpu.VMEM((rows, features), BF16),
            pltpu.VMEM((src_len, rows), F32),
            pltpu.VMEM((rows, inner), BF16),
        ],
        compiler_params=params(12),
        cost_estimate=cost(6 * rows * features * inner, 8 * features * inner),
        name="attend",
    )(idx, *parts, src, tgt, k, v, wq, wo)


def attend_backward(idx, count, parts, src, tgt, q, k, v, stats, wq, wo):
    pieces, rows, chunk, features, inner = dims(parts, wq)
    src_len = k.shape[0]
    return pl.pallas_call(
        functools.partial(backward_kernel, pieces),
        in_specs=[SMEM, SMEM] + [VMEM] * (pieces + 8),
        out_specs=[VMEM] * (2 + pieces),
        out_shape=[jax.ShapeDtypeStruct((src_len, inner), BF16)] * 2 + piece_types(rows, chunk, range(pieces)),
        scratch_shapes=[
            pltpu.VMEM((rows, features), BF16),
            pltpu.VMEM((src_len, rows), F32),
            pltpu.VMEM((rows, inner), BF16),
            pltpu.VMEM((rows, inner), BF16),
        ],
        compiler_params=params(12),
        cost_estimate=cost(8 * rows * features * inner, 8 * features * inner),
        name="attend_backward",
    )(idx, count, *parts, src, tgt, q, k, v, stats, wq, wo)


def memory_grads(idx, pieces, chunk, dk, dv, wk, wv):
    rows, inner = dk.shape
    return pl.pallas_call(
        functools.partial(memory_kernel, pieces, chunk),
        in_specs=[SMEM] + [VMEM] * 4,
        out_specs=[VMEM] * 2,
        out_shape=[
            jax.ShapeDtypeStruct((pieces, rows // 2, chunk), F32),
            jax.ShapeDtypeStruct((pieces, rows // 2, chunk), BF16),
        ],
        scratch_shapes=[
            pltpu.VMEM((pieces, rows, chunk), F32),
        ],
        compiler_params=params(12),
        cost_estimate=cost(4 * rows * chunk * pieces * inner, 4 * chunk * pieces * inner),
        name="memory_grads",
    )(idx, dk, dv, wk, wv)


def memory_grads_whole(dk, dv, wk, wv):
    return pl.pallas_call(
        memory_whole_kernel,
        in_specs=[VMEM] * 4,
        out_specs=VMEM,
        out_shape=jax.ShapeDtypeStruct((dk.shape[0], wk.shape[0]), F32),
        compiler_params=params(16),
        name="memory_grads_whole",
    )(dk, dv, wk, wv)


def swap(x, axis, step):
    size = lax.axis_size(axis)
    return lax.ppermute(x, axis, [(i, i ^ step) for i in range(size)])


def after(first, then):
    return lax.optimization_barrier((first, then))


def local(direct, memory, states, targets, w_query, w_key, w_value, w_out, src_ids, tgt_ids, counts):
    run = local_direct if direct else local_gathered
    src, tgt = src_ids.reshape(-1, 1), tgt_ids.reshape(1, -1)
    out, loss, grad_x, grad_m = run(
        memory[0],
        states[0, 0],
        targets[0, 0],
        w_query[0],
        w_key[0],
        w_value[0],
        w_out[0],
        src,
        tgt,
        counts,
    )
    return out[None, None], loss.reshape(1), grad_x[None, None], grad_m[None]


def local_gathered(mem, state, target, wq, wk, wv, wo, src, tgt, counts):
    idx = jnp.zeros((1,), jnp.int32)

    def gather(x):
        return [lax.all_gather(x, "mp", axis=1, tiled=True)]

    def scatter(x):
        return lax.psum_scatter(x, "mp", scatter_dimension=1, tiled=True)

    k, v = project_kv(idx, gather(mem), wk, wv)
    q, stats, out_part = attend(idx, gather(state), src, tgt, k, v, wq, wo)
    out_low = scatter(out_part).astype(BF16)
    dk, dv, grad_x_part = attend_backward(idx, counts, gather(target), src, tgt, q, k, v, stats, wq, wo)
    grad_m = lax.psum(scatter(memory_grads_whole(dk, dv, wk, wv)), "phase")
    valid = jnp.arange(target.shape[0])[:, None] < counts[0]
    loss_part = jnp.sum(jnp.where(valid, out_low.astype(F32) * target.astype(F32), 0.0))
    count_part = counts[0].astype(F32) / lax.axis_size("mp")
    loss_total, count_total = lax.psum((loss_part, count_part), ("dp", "mp"))
    grad_x = (scatter(grad_x_part) / count_total).astype(BF16)
    return out_low, loss_total / count_total, grad_x, (grad_m / count_total).astype(BF16)


def local_direct(mem, state, target, wq, wk, wv, wo, src, tgt, counts):
    n = lax.axis_size("mp")
    steps = range(n - 1, 0, -1)
    phase = lax.axis_index("phase")
    order = jnp.arange(n + 2, dtype=jnp.int32)
    idx = jnp.where(order < n, lax.axis_index("mp") ^ order, phase ^ (order - n))
    chunk = mem.shape[1]

    def exchange(parts):
        moved = {}
        for s in steps:
            moved[s] = swap(parts[s], "mp", s)
        return [moved[s] for s in range(1, n)]

    mem_parts = [mem] + exchange([mem] * n)
    weights = [pltpu.with_memory_space_constraint(w, pltpu.HBM) for w in (wk, wv)]
    idx, weights = after(idx, weights)
    wk, wv = load(*weights)
    mem_parts, state = after(mem_parts, state)
    state_parts = [state] + exchange([state] * n)
    k, v = project_kv(idx, mem_parts, wk, wv)
    weights = [pltpu.with_memory_space_constraint(w, pltpu.HBM) for w in (wq, wo)]
    k, weights = after(k, weights)
    wq, wo = load(*weights)
    state_parts, target = after(state_parts, target)
    target_parts = [target] + exchange([target] * n)
    q, stats, *out_parts = attend(idx, state_parts, src, tgt, k, v, wq, wo)
    out_arrived = exchange(out_parts)
    dk, dv, *grad_x_parts = attend_backward(
        idx, counts, target_parts, src, tgt, q, k, v, stats, wq, wo
    )
    grad_x_arrived = exchange(grad_x_parts)
    keep, send = memory_grads(idx, n, chunk, dk, dv, wk, wv)
    out_arrived, keep = after(out_arrived, keep)
    rows, kept = mem.shape[0], keep.shape[1]
    send_arrived = swap(send, "phase", 1)
    out_low, part = plain(
        loss_kernel,
        [jax.ShapeDtypeStruct((rows, chunk), BF16), jax.ShapeDtypeStruct(TILE, F32)],
        counts,
        out_parts[0],
        *out_arrived,
        target,
        smem=1,
    )
    terms = [part] + [swap(part, "dp", s) for s in range(1, lax.axis_size("dp"))]
    *grad_m_parts, sums = plain(
        functools.partial(join_kernel, n),
        [jax.ShapeDtypeStruct((kept, chunk), F32)]
        + [jax.ShapeDtypeStruct((kept + EXTRA, chunk), BF16)] * (n - 1)
        + [jax.ShapeDtypeStruct(TILE, F32)],
        keep,
        send_arrived,
        *terms,
    )
    grad_m_arrived = exchange(grad_m_parts)
    grad_m_half, grad_x, loss = plain(
        functools.partial(final_kernel, n),
        [
            jax.ShapeDtypeStruct((kept, chunk), BF16),
            jax.ShapeDtypeStruct((rows, chunk), BF16),
            jax.ShapeDtypeStruct(TILE, F32),
        ],
        sums,
        grad_m_parts[0],
        *grad_m_arrived,
        grad_x_parts[0],
        *grad_x_arrived,
    )
    grad_m_other = swap(grad_m_half, "phase", 1)
    first = phase == 0
    grad_m = jnp.concatenate(
        [jnp.where(first, grad_m_half, grad_m_other), jnp.where(first, grad_m_other, grad_m_half)], axis=0
    )
    return out_low, loss[0, 0], grad_x, grad_m


def power_of_two(size):
    return size & (size - 1) == 0


def solution(mesh):
    sizes = mesh.shape
    placed = (
        P("dp", None, "mp"),
        P("phase", "dp", None, "mp"),
        P("phase", "dp", None, "mp"),
        P("phase", None, "mp"),
        P("phase", None, "mp"),
        P("phase", None, "mp"),
        P("phase", "mp", None),
        P("dp", None),
        P("dp", None),
        P("dp"),
    )
    direct = 1 < sizes["mp"] <= 4 and power_of_two(sizes["mp"]) and power_of_two(sizes["dp"]) and sizes["phase"] == 2
    return jax.shard_map(
        functools.partial(local, direct),
        mesh=mesh,
        in_specs=placed,
        out_specs=(
            P("phase", "dp", None, "mp"),
            P("phase"),
            P("phase", "dp", None, "mp"),
            P("dp", None, "mp"),
        ),
        check_vma=False,
    )
```

time: 246 us -> 127 us (0.52)
  blocking collectives: 82.2 us -> 0 us
  matrix products: 76.1 us -> 0 us
  Pallas kernels: 0 us -> 57.7 us
  starting transfers between devices: 0.38 us -> 31.4 us
  waiting for transfers between devices: 49.1 us -> 27.2 us
  between operations: 17 us -> 1.47 us
  other arithmetic: 8.67 us -> 0.68 us
  local copies, waits for them, and re-layouts: 11.9 us -> 7.99 us
    dot_general x13 -> x0, matrix products: 68.5 us -> none  [the longest x1 7.11 us: local(): jnp.einsum('btd,kd->btk', grad_out, wo, preferred_element_type=jnp.float32)]
    pallas_call x0 -> x9, Pallas kernels: none -> 57.7 us  [the longest x1 20.2 us: attend_backward(): pl.pallas_call(functools.partial(backward_kernel, pieces), in_specs=[SMEM...]
    all_gather x3 -> x0, blocking collectives: 49.6 us -> none  [the longest x1 17.6 us: local(): lax.all_gather(memory, 'mp', axis=2, tiled=True)]
    reduce_scatter x3 -> x0, waiting for transfers between devices: 34.5 us -> none  [the longest x1 28.1 us: local(): out_sum = lax.psum_scatter(out_part, 'mp', scatter_dimension=2, tiled=True)]
    psum x1 -> x0, blocking collectives: 32.6 us -> none  [local(): lax.psum((loss_part, count_local / lax.axis_size('mp')), ('dp', 'mp'))]
    ppermute x0 -> x23, starting transfers between devices: none -> 31.4 us  [swap(): return lax.ppermute(x, axis, [(i, i ^ step) for i in range(size)])]
    ppermute x0 -> x23, waiting for transfers between devices: none -> 27.2 us  [swap(): return lax.ppermute(x, axis, [(i, i ^ step) for i in range(size)])]
    psum x1 -> x0, waiting for transfers between devices: 14.5 us -> none  [local(): grad_mem = lax.psum(grad_m, 'phase')]
  transfers between devices with their start and end apart: 4 -> 23, of which waited for: 3 -> 9; matrix products, arithmetic and copies ran while one was open for 11% -> 1% of each run, Pallas kernels for 0% -> 25%
where the time goes in v2:
time: 127 us; the launch traced here: 126 us
  Pallas kernels  57.7 us (45%)
  starting transfers between devices  31.4 us (25%)
  waiting for transfers between devices  27.2 us (21%)
  local copies, waits for them, and re-layouts  7.99 us (6%)
  between operations  1.47 us (1%)
    ppermute x23, starting transfers between devices, swap(): return lax.ppermute(x, axis, [(i, i ^ step) for i in range(size)])  31.4 us
    ppermute x23, waiting for transfers between devices, swap(): return lax.ppermute(x, axis, [(i, i ^ step) for i in range(size)])  27.2 us
    pallas_call x1, Pallas kernels, attend_backward(): pl.pallas_call(functools.partial(backward_kernel, pieces), in_specs=[SMEM...  20.2 us
    pallas_call x1, Pallas kernels, attend(): pl.pallas_call(functools.partial(forward_kernel, pieces), in_specs=[SMEM]...  12.6 us
    pallas_call x2, Pallas kernels, load(): pl.pallas_call(load_kernel, in_specs=[HBM] * len(weights), out_specs=[VME...  11.9 us
    unnamed x12, local copies, waits for them, and re-layouts  6.67 us
    pallas_call x1, Pallas kernels, project_kv(): pl.pallas_call(functools.partial(kv_kernel, pieces), in_specs=[SMEM] + [V...  6.34 us
    pallas_call x1, Pallas kernels, memory_grads(): pl.pallas_call(functools.partial(memory_kernel, pieces, chunk), in_specs=...  5.14 us
  transfers between devices with their start and end apart: 23, of which 9 were waited for; matrix products, arithmetic and copies ran while one was open for 1% of the time, Pallas kernels for 25%

profile of v2, /device:TPU:0, one launch (start us, length us, event | category | flops | bytes accessed | tf_op | source)
XLA Modules:
  0.0 126.4 jit_solution(16205530113983617816)
XLA Ops:
  0.6 3.1 %collective-permute-start = (bf16[256,256]{1,0:T(8,128)(2,1)}, bf16[256,256]{1,0:T(8,128)(2,1)S(1)}, u32[]{:S(2)}, u32[]{:S(2)}) collective-permute-start(bf16[256,256]{1,0:T(8,128)(2,1)} %bitcast.13), channel_id=1, source_target_pairs={{0,1},{1,0},{2,3},{3,2},{4,5},{5,4},{6,7},{7,6},{8,9},{9,8},{10,11... | collective-permute-start | bytes 393224 | tf_op jit(solution)/shard_map/ppermute | solution.py:373
  3.7 2.6 %collective-permute-start.1 = (bf16[256,256]{1,0:T(8,128)(2,1)}, bf16[256,256]{1,0:T(8,128)(2,1)S(1)}, u32[]{:S(2)}, u32[]{:S(2)}) collective-permute-start(bf16[256,256]{1,0:T(8,128)(2,1)} %bitcast.14), channel_id=1, source_target_pairs={{0,2},{1,3},{2,0},{3,1},{4,6},{5,7},{6,4},{7,5},{8,10},{9,11},{10,... | collective-permute-start | bytes 393224 | tf_op jit(solution)/shard_map/ppermute | solution.py:373
  7.8 6.0 %load.2 = (bf16[1024,4096]{1,0:T(8,128)(2,1)S(1)}, bf16[1024,4096]{1,0:T(8,128)(2,1)S(1)}) custom-call(bf16[1024,4096]{1,0:T(8,128)(2,1)} %bitcast.26, bf16[1024,4096]{1,0:T(8,128)(2,1)} %bitcast.27), custom_call_target="tpu_custom_call" | custom-call | bytes 16777216 | tf_op jit(solution)/shard_map/load/pallas_call | solution.py:260
  13.8 3.0 %collective-permute-done.1.refs_2_ = bf16[256,256]{1,0:T(8,128)(2,1)S(1)} collective-permute-done((bf16[256,256]{1,0:T(8,128)(2,1)}, bf16[256,256]{1,0:T(8,128)(2,1)S(1)}, u32[]{:S(2)}, u32[]{:S(2)}) %collective-permute-start.1) | collective-permute-done | bytes 131104 | tf_op jit(solution)/shard_map/ppermute | solution.py:373
  16.8 2.0 %collective-permute-start.3 = (bf16[256,256]{1,0:T(8,128)(2,1)S(1)}, bf16[256,256]{1,0:T(8,128)(2,1)S(1)}, u32[]{:S(2)}, u32[]{:S(2)}) collective-permute-start(bf16[256,256]{1,0:T(8,128)(2,1)S(1)} %bitcast.22), channel_id=1, source_target_pairs={{0,1},{1,0},{2,3},{3,2},{4,5},{5,4},{6,7},{7,6},{8,9},{9,8},{10,11... | collective-permute-start | bytes 393224 | tf_op jit(solution)/shard_map/ppermute | solution.py:373
  21.3 6.3 %project_kv.1 = (bf16[256,4096]{1,0:T(8,128)(2,1)S(1)}, bf16[256,4096]{1,0:T(8,128)(2,1)S(1)}) custom-call(s32[6]{0:T(128)S(1)} %compare_select_fusion.idx, bf16[256,256]{1,0:T(8,128)(2,1)S(1)} %bitcast.16, bf16[256,256]{1,0:T(8,128)(2,1)S(1)} %collective-permute-done.refs_1_, bf16[256,256]{1,0:T(8,128)(2,1)S(1)} %collective-permute-done.1.refs_2_, ...), custom_call_target="tpu_custom_call" | custom-call | flops 4294967296 | bytes 16777216 | tf_op jit(solution)/shard_map/project_kv/pallas_call | solution.py:284
  27.7 6.0 %load.3 = (bf16[1024,4096]{1,0:T(8,128)(2,1)S(1)}, bf16[4096,1024]{1,0:T(8,128)(2,1)S(1)}) custom-call(bf16[1024,4096]{1,0:T(8,128)(2,1)} %bitcast.28, bf16[4096,1024]{1,0:T(8,128)(2,1)} %bitcast.29), custom_call_target="tpu_custom_call" | custom-call | bytes 16777216 | tf_op jit(solution)/shard_map/load/pallas_call | solution.py:260
  33.7 3.3 %copy-done.2 = bf16[1024,4096]{1,0:T(8,128)(2,1)} copy-done((bf16[1024,4096]{1,0:T(8,128)(2,1)}, bf16[1024,4096]{1,0:T(8,128)(2,1)S(1)}, u32[]{:S(2)}) %copy-start.2) | copy-done | bytes 8388632
  38.1 1.9 %collective-permute-start.10 = (bf16[256,256]{1,0:T(8,128)(2,1)S(1)}, bf16[256,256]{1,0:T(8,128)(2,1)S(1)}, u32[]{:S(2)}, u32[]{:S(2)}) collective-permute-start(bf16[256,256]{1,0:T(8,128)(2,1)S(1)} %bitcast.18), channel_id=1, source_target_pairs={{0,2},{1,3},{2,0},{3,1},{4,6},{5,7},{6,4},{7,5},{8,10},{9,11},{10,... | collective-permute-start | bytes 393224 | tf_op jit(solution)/shard_map/ppermute | solution.py:373
  41.4 3.4 %copy-done.3 = bf16[1024,4096]{1,0:T(8,128)(2,1)S(1)} copy-done((bf16[1024,4096]{1,0:T(8,128)(2,1)S(1)}, bf16[1024,4096]{1,0:T(8,128)(2,1)}, u32[]{:S(2)}) %copy-start.3) | copy-done | bytes 8388632
  44.8 12.6 %attend.1 = (bf16[256,4096]{1,0:T(8,128)(2,1)S(1)}, f32[32,2,256]{2,1,0:T(2,128)S(1)}, f32[256,256]{1,0:T(8,128)S(1)}, bf16[256,256]{1,0:T(8,128)(2,1)S(1)}, bf1...) custom-call(s32[6]{0:T(128)S(1)} %compare_select_fusion.idx, bf16[256,256]{1,0:T(8,128)(2,1)S(1)} %bitcast.25, ...), custom_call_target="tpu_custom_call" | custom-call | flops 6442450944 | bytes 33554432 | tf_op jit(solution)/shard_map/attend/pallas_call | solution.py:301
  57.4 20.2 %attend_backward.1 = (bf16[256,4096]{1,0:T(8,128)(2,1)S(1)}, bf16[256,4096]{1,0:T(8,128)(2,1)S(1)}, f32[256,256]{1,0:T(8,128)S(1)}, bf16[256,256]{1,0:T(8,128)(2...) custom-call(s32[6]{0:T(128)S(1)} %compare_select_fusion.idx, s32[1]{0:T(128)S(6)} %copy.16.count, ...), custom_call_target="tpu_custom_call" | custom-call | flops 8589934592 | bytes 33554432 | tf_op jit(solution)/shard_map/attend_backward/pallas_call | solution.py:324
  77.6 5.1 %memory_grads.1 = (f32[4,128,256]{2,1,0:T(8,128)S(1)}, bf16[4,128,256]{2,1,0:T(8,128)(2,1)S(1)}) custom-call(s32[6]{0:T(128)S(1)} %compare_select_fusion.idx, bf16[256,4096]{1,0:T(8,128)(2,1)S(1)} %get-tuple-element.82.dk, bf16[256,4096]{1,0:T(8,128)(2,1)S(1)} %get-tuple-element.83.dv, bf16[1024,4096]{1,0:T(8,128)(2,1)S(1)} %get-tuple-element.66.refs_4_.wk, ...), custom_call_target="tpu_custom_call" | custom-call | flops 4294967296 | bytes 16777216 | tf_op jit(solution)/shard_map/memory_grads/pallas_call | solution.py:343
  82.7 1.6 %collective-permute-start.12 = (bf16[4,128,256]{2,1,0:T(8,128)(2,1)S(1)}, bf16[4,128,256]{2,1,0:T(8,128)(2,1)S(1)}, u32[]{:S(2)}, u32[]{:S(2)}) collective-permute-start(bf16[4,128,256]{2,1,0:T(8,128)(2,1)S(1)} %get-tuple-element.90), channel_id=1, source_target_pairs={{0,16},{16,0},{1,17},{17,1},{2,18},{18,2},{3,19},{19,3},{4,20},{20... | collective-permute-start | bytes 786440 | tf_op jit(solution)/shard_map/ppermute | solution.py:373
  84.4 2.8 %collective-permute-start.7 = (bf16[256,256]{1,0:T(8,128)(2,1)S(1)}, bf16[256,256]{1,0:T(8,128)(2,1)S(1)}, u32[]{:S(2)}, u32[]{:S(2)}) collective-permute-start(bf16[256,256]{1,0:T(8,128)(2,1)S(1)} %get-tuple-element.77), channel_id=1, source_target_pairs={{0,2},{1,3},{2,0},{3,1},{4,6},{5,7},{6,4},{7,5},{8,10},{9,11},{10,... | collective-permute-start | bytes 393224 | tf_op jit(solution)/shard_map/ppermute | solution.py:373
  88.7 5.2 %collective-permute-done.6.refs_0_ = bf16[256,256]{1,0:T(8,128)(2,1)S(1)} collective-permute-done((bf16[256,256]{1,0:T(8,128)(2,1)S(1)}, bf16[256,256]{1,0:T(8,128)(2,1)S(1)}, u32[]{:S(2)}, u32[]{:S(2)}) %collective-permute-start.6) | collective-permute-done | bytes 131104 | tf_op jit(solution)/shard_map/ppermute | solution.py:373
  93.9 3.4 %collective-permute-done.7.refs_1_ = bf16[256,256]{1,0:T(8,128)(2,1)S(1)} collective-permute-done((bf16[256,256]{1,0:T(8,128)(2,1)S(1)}, bf16[256,256]{1,0:T(8,128)(2,1)S(1)}, u32[]{:S(2)}, u32[]{:S(2)}) %collective-permute-start.7) | collective-permute-done | bytes 131104 | tf_op jit(solution)/shard_map/ppermute | solution.py:373
  97.3 2.5 %collective-permute-start.21 = (bf16[256,256]{1,0:T(8,128)(2,1)S(1)}, bf16[256,256]{1,0:T(8,128)(2,1)S(1)}, u32[]{:S(2)}, u32[]{:S(2)}) collective-permute-start(bf16[256,256]{1,0:T(8,128)(2,1)S(1)} %get-tuple-element.100), channel_id=1, source_target_pairs={{0,3},{1,2},{2,1},{3,0},{4,7},{5,6},{6,5},{7,4},{8,11},{9,10},{10,... | collective-permute-start | bytes 393224 | tf_op jit(solution)/shard_map/ppermute | solution.py:373
  103.2 2.1 %collective-permute-done.14.refs_2_ = f32[8,128]{1,0:T(8,128)S(1)} collective-permute-done((f32[8,128]{1,0:T(8,128)S(1)}, f32[8,128]{1,0:T(8,128)S(1)}, u32[]{:S(2)}, u32[]{:S(2)}) %collective-permute-start.14) | collective-permute-done | bytes 4128 | tf_op jit(solution)/shard_map/ppermute | solution.py:373
  105.8 2.6 %collective-permute-done.15.refs_3_ = f32[8,128]{1,0:T(8,128)S(1)} collective-permute-done((f32[8,128]{1,0:T(8,128)S(1)}, f32[8,128]{1,0:T(8,128)S(1)}, u32[]{:S(2)}, u32[]{:S(2)}) %collective-permute-start.15) | collective-permute-done | bytes 4128 | tf_op jit(solution)/shard_map/ppermute | solution.py:373
  108.4 3.5 %collective-permute-start.16 = (bf16[144,256]{1,0:T(8,128)(2,1)S(1)}, bf16[144,256]{1,0:T(8,128)(2,1)S(1)}, u32[]{:S(2)}, u32[]{:S(2)}) collective-permute-start(bf16[144,256]{1,0:T(8,128)(2,1)S(1)} %get-tuple-element.94), channel_id=1, source_target_pairs={{0,1},{1,0},{2,3},{3,2},{4,5},{5,4},{6,7},{7,6},{8,9},{9,8},{10,11... | collective-permute-start | bytes 221192 | tf_op jit(solution)/shard_map/ppermute | solution.py:373
  112.8 1.5 %collective-permute-start.18 = (bf16[144,256]{1,0:T(8,128)(2,1)S(1)}, bf16[144,256]{1,0:T(8,128)(2,1)S(1)}, u32[]{:S(2)}, u32[]{:S(2)}) collective-permute-start(bf16[144,256]{1,0:T(8,128)(2,1)S(1)} %get-tuple-element.96), channel_id=1, source_target_pairs={{0,3},{1,2},{2,1},{3,0},{4,7},{5,6},{6,5},{7,4},{8,11},{9,10},{10,... | collective-permute-start | bytes 221192 | tf_op jit(solution)/shard_map/ppermute | solution.py:373
  114.5 6.2 %collective-permute-done.17.refs_2_ = bf16[144,256]{1,0:T(8,128)(2,1)S(1)} collective-permute-done((bf16[144,256]{1,0:T(8,128)(2,1)S(1)}, bf16[144,256]{1,0:T(8,128)(2,1)S(1)}, u32[]{:S(2)}, u32[]{:S(2)}) %collective-permute-start.17) | collective-permute-done | bytes 73760 | tf_op jit(solution)/shard_map/ppermute | solution.py:373
  122.5 3.3 %collective-permute-done.22 = bf16[128,256]{1,0:T(8,128)(2,1)S(1)} collective-permute-done((bf16[128,256]{1,0:T(8,128)(2,1)S(1)}, bf16[128,256]{1,0:T(8,128)(2,1)S(1)}, u32[]{:S(2)}, u32[]{:S(2)}) %collective-permute-start.22) | collective-permute-done | bytes 65568 | tf_op jit(solution)/shard_map/ppermute | solution.py:373
  (48 shorter events, 14.9 us)
Async XLA Ops:
  0.6 13.2 %collective-permute-start = (bf16[256,256]{1,0:T(8,128)(2,1)}, bf16[256,256]{1,0:T(8,128)(2,1)S(1)}, u32[]{:S(2)}, u32[]{:S(2)}) collective-permute-start(bf16[256,256]{1,0:T(8,128)(2,1)} %bitcast.13), channel_id=1, source_target_pairs={{0,1},{1,0},{2,3},{3,2},{4,5},{5,4},{6,7},{7,6},{8,9},{9,8},{10,11... | collective-permute-start | bytes 393224 | tf_op jit(solution)/shard_map/ppermute | solution.py:373
  3.7 13.1 %collective-permute-start.1 = (bf16[256,256]{1,0:T(8,128)(2,1)}, bf16[256,256]{1,0:T(8,128)(2,1)S(1)}, u32[]{:S(2)}, u32[]{:S(2)}) collective-permute-start(bf16[256,256]{1,0:T(8,128)(2,1)} %bitcast.14), channel_id=1, source_target_pairs={{0,2},{1,3},{2,0},{3,1},{4,6},{5,7},{6,4},{7,5},{8,10},{9,11},{10,... | collective-permute-start | bytes 393224 | tf_op jit(solution)/shard_map/ppermute | solution.py:373
  6.3 10.5 %collective-permute-start.2 = (bf16[256,256]{1,0:T(8,128)(2,1)}, bf16[256,256]{1,0:T(8,128)(2,1)S(1)}, u32[]{:S(2)}, u32[]{:S(2)}) collective-permute-start(bf16[256,256]{1,0:T(8,128)(2,1)} %bitcast.15), channel_id=1, source_target_pairs={{0,3},{1,2},{2,1},{3,0},{4,7},{5,6},{6,5},{7,4},{8,11},{9,10},{10,... | collective-permute-start | bytes 393224 | tf_op jit(solution)/shard_map/ppermute | solution.py:373
  16.8 20.1 %collective-permute-start.3 = (bf16[256,256]{1,0:T(8,128)(2,1)S(1)}, bf16[256,256]{1,0:T(8,128)(2,1)S(1)}, u32[]{:S(2)}, u32[]{:S(2)}) collective-permute-start(bf16[256,256]{1,0:T(8,128)(2,1)S(1)} %bitcast.22), channel_id=1, source_target_pairs={{0,1},{1,0},{2,3},{3,2},{4,5},{5,4},{6,7},{7,6},{8,9},{9,8},{10,11... | collective-permute-start | bytes 393224 | tf_op jit(solution)/shard_map/ppermute | solution.py:373
  18.9 18.1 %collective-permute-start.4 = (bf16[256,256]{1,0:T(8,128)(2,1)S(1)}, bf16[256,256]{1,0:T(8,128)(2,1)S(1)}, u32[]{:S(2)}, u32[]{:S(2)}) collective-permute-start(bf16[256,256]{1,0:T(8,128)(2,1)S(1)} %bitcast.23), channel_id=1, source_target_pairs={{0,2},{1,3},{2,0},{3,1},{4,6},{5,7},{6,4},{7,5},{8,10},{9,11},{10,... | collective-permute-start | bytes 393224 | tf_op jit(solution)/shard_map/ppermute | solution.py:373
  19.9 17.1 %collective-permute-start.5 = (bf16[256,256]{1,0:T(8,128)(2,1)S(1)}, bf16[256,256]{1,0:T(8,128)(2,1)S(1)}, u32[]{:S(2)}, u32[]{:S(2)}) collective-permute-start(bf16[256,256]{1,0:T(8,128)(2,1)S(1)} %bitcast.24), channel_id=1, source_target_pairs={{0,3},{1,2},{2,1},{3,0},{4,7},{5,6},{6,5},{7,4},{8,11},{9,10},{10,... | collective-permute-start | bytes 393224 | tf_op jit(solution)/shard_map/ppermute | solution.py:373
  27.7 13.7 %copy-start.5 = (s32[1,256]{1,0:T(1,128)S(1)}, s32[1,256]{1,0:T(1,128)}, u32[]{:S(2)}) copy-start(s32[1,256]{1,0:T(1,128)} %refs_5_.3) | copy-start | bytes 3076
  37.0 20.4 %collective-permute-start.9 = (bf16[256,256]{1,0:T(8,128)(2,1)S(1)}, bf16[256,256]{1,0:T(8,128)(2,1)S(1)}, u32[]{:S(2)}, u32[]{:S(2)}) collective-permute-start(bf16[256,256]{1,0:T(8,128)(2,1)S(1)} %bitcast.17), channel_id=1, source_target_pairs={{0,1},{1,0},{2,3},{3,2},{4,5},{5,4},{6,7},{7,6},{8,9},{9,8},{10,11... | collective-permute-start | bytes 393224 | tf_op jit(solution)/shard_map/ppermute | solution.py:373
  38.1 19.3 %collective-permute-start.10 = (bf16[256,256]{1,0:T(8,128)(2,1)S(1)}, bf16[256,256]{1,0:T(8,128)(2,1)S(1)}, u32[]{:S(2)}, u32[]{:S(2)}) collective-permute-start(bf16[256,256]{1,0:T(8,128)(2,1)S(1)} %bitcast.18), channel_id=1, source_target_pairs={{0,2},{1,3},{2,0},{3,1},{4,6},{5,7},{6,4},{7,5},{8,10},{9,11},{10,... | collective-permute-start | bytes 393224 | tf_op jit(solution)/shard_map/ppermute | solution.py:373
  40.0 17.4 %collective-permute-start.11 = (bf16[256,256]{1,0:T(8,128)(2,1)S(1)}, bf16[256,256]{1,0:T(8,128)(2,1)S(1)}, u32[]{:S(2)}, u32[]{:S(2)}) collective-permute-start(bf16[256,256]{1,0:T(8,128)(2,1)S(1)} %bitcast.19), channel_id=1, source_target_pairs={{0,3},{1,2},{2,1},{3,0},{4,7},{5,6},{6,5},{7,4},{8,11},{9,10},{10,... | collective-permute-start | bytes 393224 | tf_op jit(solution)/shard_map/ppermute | solution.py:373
  82.7 25.6 %collective-permute-start.12 = (bf16[4,128,256]{2,1,0:T(8,128)(2,1)S(1)}, bf16[4,128,256]{2,1,0:T(8,128)(2,1)S(1)}, u32[]{:S(2)}, u32[]{:S(2)}) collective-permute-start(bf16[4,128,256]{2,1,0:T(8,128)(2,1)S(1)} %get-tuple-element.90), channel_id=1, source_target_pairs={{0,16},{16,0},{1,17},{17,1},{2,18},{18,2},{3,19},{19,3},{4,20},{20... | collective-permute-start | bytes 786440 | tf_op jit(solution)/shard_map/ppermute | solution.py:373
  84.3 9.6 %collective-permute-start.6 = (bf16[256,256]{1,0:T(8,128)(2,1)S(1)}, bf16[256,256]{1,0:T(8,128)(2,1)S(1)}, u32[]{:S(2)}, u32[]{:S(2)}) collective-permute-start(bf16[256,256]{1,0:T(8,128)(2,1)S(1)} %get-tuple-element.76), channel_id=1, source_target_pairs={{0,1},{1,0},{2,3},{3,2},{4,5},{5,4},{6,7},{7,6},{8,9},{9,8},{10,11... | collective-permute-start | bytes 393224 | tf_op jit(solution)/shard_map/ppermute | solution.py:373
  84.4 12.9 %collective-permute-start.7 = (bf16[256,256]{1,0:T(8,128)(2,1)S(1)}, bf16[256,256]{1,0:T(8,128)(2,1)S(1)}, u32[]{:S(2)}, u32[]{:S(2)}) collective-permute-start(bf16[256,256]{1,0:T(8,128)(2,1)S(1)} %get-tuple-element.77), channel_id=1, source_target_pairs={{0,2},{1,3},{2,0},{3,1},{4,6},{5,7},{6,4},{7,5},{8,10},{9,11},{10,... | collective-permute-start | bytes 393224 | tf_op jit(solution)/shard_map/ppermute | solution.py:373
  87.3 12.5 %collective-permute-start.8 = (bf16[256,256]{1,0:T(8,128)(2,1)S(1)}, bf16[256,256]{1,0:T(8,128)(2,1)S(1)}, u32[]{:S(2)}, u32[]{:S(2)}) collective-permute-start(bf16[256,256]{1,0:T(8,128)(2,1)S(1)} %get-tuple-element.78), channel_id=1, source_target_pairs={{0,3},{1,2},{2,1},{3,0},{4,7},{5,6},{6,5},{7,4},{8,11},{9,10},{10,... | collective-permute-start | bytes 393224 | tf_op jit(solution)/shard_map/ppermute | solution.py:373
  88.7 24.1 %collective-permute-start.19 = (bf16[256,256]{1,0:T(8,128)(2,1)S(1)}, bf16[256,256]{1,0:T(8,128)(2,1)S(1)}, u32[]{:S(2)}, u32[]{:S(2)}) collective-permute-start(bf16[256,256]{1,0:T(8,128)(2,1)S(1)} %get-tuple-element.98), channel_id=1, source_target_pairs={{0,1},{1,0},{2,3},{3,2},{4,5},{5,4},{6,7},{7,6},{8,9},{9,8},{10,11... | collective-permute-start | bytes 393224 | tf_op jit(solution)/shard_map/ppermute | solution.py:373
  93.9 20.4 %collective-permute-start.20 = (bf16[256,256]{1,0:T(8,128)(2,1)S(1)}, bf16[256,256]{1,0:T(8,128)(2,1)S(1)}, u32[]{:S(2)}, u32[]{:S(2)}) collective-permute-start(bf16[256,256]{1,0:T(8,128)(2,1)S(1)} %get-tuple-element.99), channel_id=1, source_target_pairs={{0,2},{1,3},{2,0},{3,1},{4,6},{5,7},{6,4},{7,5},{8,10},{9,11},{10,... | collective-permute-start | bytes 393224 | tf_op jit(solution)/shard_map/ppermute | solution.py:373
  97.3 17.0 %collective-permute-start.21 = (bf16[256,256]{1,0:T(8,128)(2,1)S(1)}, bf16[256,256]{1,0:T(8,128)(2,1)S(1)}, u32[]{:S(2)}, u32[]{:S(2)}) collective-permute-start(bf16[256,256]{1,0:T(8,128)(2,1)S(1)} %get-tuple-element.100), channel_id=1, source_target_pairs={{0,3},{1,2},{2,1},{3,0},{4,7},{5,6},{6,5},{7,4},{8,11},{9,10},{10,... | collective-permute-start | bytes 393224 | tf_op jit(solution)/shard_map/ppermute | solution.py:373
  100.5 1.2 collective-permute-start.13
  101.7 3.6 %collective-permute-start.14 = (f32[8,128]{1,0:T(8,128)S(1)}, f32[8,128]{1,0:T(8,128)S(1)}, u32[]{:S(2)}, u32[]{:S(2)}) collective-permute-start(f32[8,128]{1,0:T(8,128)S(1)} %get-tuple-element.91.refs_0_), channel_id=1, source_target_pairs={{0,8},{4,12},{8,0},{12,4},{1,9},{5,13},{9,1},{13,5},{2,10},{6,14},... | collective-permute-start | bytes 12296 | tf_op jit(solution)/shard_map/ppermute | solution.py:373
  105.3 3.0 %collective-permute-start.15 = (f32[8,128]{1,0:T(8,128)S(1)}, f32[8,128]{1,0:T(8,128)S(1)}, u32[]{:S(2)}, u32[]{:S(2)}) collective-permute-start(f32[8,128]{1,0:T(8,128)S(1)} %get-tuple-element.91.refs_0_), channel_id=1, source_target_pairs={{0,12},{4,8},{8,4},{12,0},{1,13},{5,9},{9,5},{13,1},{2,14},{6,10},... | collective-permute-start | bytes 12296 | tf_op jit(solution)/shard_map/ppermute | solution.py:373
  108.4 6.1 %collective-permute-start.16 = (bf16[144,256]{1,0:T(8,128)(2,1)S(1)}, bf16[144,256]{1,0:T(8,128)(2,1)S(1)}, u32[]{:S(2)}, u32[]{:S(2)}) collective-permute-start(bf16[144,256]{1,0:T(8,128)(2,1)S(1)} %get-tuple-element.94), channel_id=1, source_target_pairs={{0,1},{1,0},{2,3},{3,2},{4,5},{5,4},{6,7},{7,6},{8,9},{9,8},{10,11... | collective-permute-start | bytes 221192 | tf_op jit(solution)/shard_map/ppermute | solution.py:373
  111.9 8.8 %collective-permute-start.17 = (bf16[144,256]{1,0:T(8,128)(2,1)S(1)}, bf16[144,256]{1,0:T(8,128)(2,1)S(1)}, u32[]{:S(2)}, u32[]{:S(2)}) collective-permute-start(bf16[144,256]{1,0:T(8,128)(2,1)S(1)} %get-tuple-element.95), channel_id=1, source_target_pairs={{0,2},{1,3},{2,0},{3,1},{4,6},{5,7},{6,4},{7,5},{8,10},{9,11},{10,... | collective-permute-start | bytes 221192 | tf_op jit(solution)/shard_map/ppermute | solution.py:373
  112.8 7.9 %collective-permute-start.18 = (bf16[144,256]{1,0:T(8,128)(2,1)S(1)}, bf16[144,256]{1,0:T(8,128)(2,1)S(1)}, u32[]{:S(2)}, u32[]{:S(2)}) collective-permute-start(bf16[144,256]{1,0:T(8,128)(2,1)S(1)} %get-tuple-element.96), channel_id=1, source_target_pairs={{0,3},{1,2},{2,1},{3,0},{4,7},{5,6},{6,5},{7,4},{8,11},{9,10},{10,... | collective-permute-start | bytes 221192 | tf_op jit(solution)/shard_map/ppermute | solution.py:373
  121.5 4.3 %collective-permute-start.22 = (bf16[128,256]{1,0:T(8,128)(2,1)S(1)}, bf16[128,256]{1,0:T(8,128)(2,1)S(1)}, u32[]{:S(2)}, u32[]{:S(2)}) collective-permute-start(bf16[128,256]{1,0:T(8,128)(2,1)S(1)} %get-tuple-element.103), channel_id=1, source_target_pairs={{0,16},{16,0},{1,17},{17,1},{2,18},{18,2},{3,19},{19,3},{4,20},{20... | collective-permute-start | bytes 196616 | tf_op jit(solution)/shard_map/ppermute | solution.py:373
  (5 other events, 38.5 us)
